TPU v7x, 128 devices: a whole 4x4x4 slice. The times are simulated.
128 devices in a mesh: space: 32 (over y, x, core), snap: 4 (over z).
Axes of the slice: x: 4, y: 4, z: 4, core: 2. Of those that a mesh axis runs over, the one named last changes fastest.
Arguments:
- owned_x: bfloat16 [4096, 128, 512], P('space', None, 'snap'), may hold values from -600 to 600
- owned_y: bfloat16 [4096, 128, 512], P('space', None, 'snap'), may hold values from -6 to 6
- patch_dest: int32 [4096], P('space'), may hold values from -1 to 2047, as said below
Outputs:
- q_basis: float32 [2048, 128, 512], P('space', 'snap')
- r_factor: float32 [512, 512], replicated
- projection: float32 [512, 512], replicated
Inputs may be any that keep to these rules, and one draw needn't show every extreme that they name: `patch_dest`: every row block 0 to 2047 is named by exactly one slot; -1 marks an empty slot. The 128 slots of one owner (one aligned block of 128 slots) name at most 4 row blocks of any one slab d * 64 to (d + 1) * 64 - 1, and some owner names exactly 4 of every slab.
All inputs are finite; a program needn't handle non-finite values.
Results may differ from a plain program's by a relative error of at most 0.0003.
Values may be sent and summed in bfloat16 or wider, within the bound.
A program may use at most 128 MiB of HBM per device.

v0:
```python
import math

import jax
import jax.numpy as jnp
from jax import lax
from jax.sharding import PartitionSpec as P

PATCH = 128
BLK_DEV = 64


def in_order(pieces, dim):
    pieces = jnp.moveaxis(pieces, 0, dim)
    shape = pieces.shape
    return pieces.reshape(*shape[:dim], shape[dim] * shape[dim + 1], *shape[dim + 2 :])


def from_everyone(array, axis):
    copies = jnp.broadcast_to(array, (lax.axis_size(axis), *array.shape))
    return lax.all_to_all(copies, axis, split_axis=0, concat_axis=0, tiled=True)


def collect(array, axis, dim):
    return in_order(from_everyone(array, axis), dim)


def slab_ranks(destination, per_slab):
    target = jnp.where(destination >= 0, destination // per_slab, -1)
    slot_count = destination.shape[-1]
    same_slab = target[..., :, None] == target[..., None, :]
    before = lax.broadcasted_iota(jnp.int32, (slot_count, slot_count), 1) < lax.broadcasted_iota(
        jnp.int32, (slot_count, slot_count), 0
    )
    order_rank = jnp.sum((same_slab & before).astype(jnp.int32), axis=-1)
    return (target, order_rank)


def send_table(destination, per_slab, slab_count, capacity):
    target, order_rank = slab_ranks(destination, per_slab)
    slot_count = destination.shape[0]
    where_to = jnp.where(target >= 0, target * capacity + order_rank, slab_count * capacity)
    start_table = jnp.full((slab_count * capacity,), slot_count, jnp.int32)
    return start_table.at[where_to].set(jnp.arange(slot_count, dtype=jnp.int32), mode="drop")


def arrival_index(all_lists, per_slab, capacity, my_slab):
    slot_count = all_lists.shape[1]
    target, order_rank = slab_ranks(all_lists, per_slab)
    wanted = my_slab * per_slab + jnp.arange(per_slab, dtype=jnp.int32)
    matches = all_lists.reshape(-1)[None, :] == wanted[:, None]
    located = jnp.argmax(matches, axis=1)
    source = located // slot_count
    return source * capacity + order_rank.reshape(-1)[located]


def pick_rows(payload, indices):
    return jnp.take(payload, indices, axis=0, mode="fill", fill_value=0)


def body(owned_x, owned_y, patch_dest):
    slab_count = lax.axis_size("space")
    slot_count = patch_dest.shape[0]
    capacity = slot_count // slab_count
    my_slab = lax.axis_index("space")
    all_lists = collect(patch_dest, "space", 0)
    outgoing_table = send_table(patch_dest, BLK_DEV, slab_count, capacity)
    received_at = arrival_index(
        all_lists.reshape(slab_count, slot_count), BLK_DEV, capacity, my_slab
    )
    rows_total = slab_count * BLK_DEV * PATCH
    contract = (((0,), (0,)), ((), ()))
    block_x, block_y = (
        lax.all_to_all(owned_x, "snap", split_axis=1, concat_axis=2, tiled=True),
        lax.all_to_all(owned_y, "snap", split_axis=1, concat_axis=2, tiled=True),
    )
    width = block_x.shape[-1]
    used = patch_dest >= 0
    kept_x = jnp.where(used[:, None, None], block_x, jnp.zeros_like(block_x))
    local_cross = lax.dot_general(
        kept_x.reshape(-1, width),
        block_y.reshape(-1, width),
        contract,
        preferred_element_type=jnp.float32,
    )
    moved_x = lax.all_to_all(
        pick_rows(block_x, outgoing_table), "space", split_axis=0, concat_axis=0, tiled=True
    )
    slab_x = jnp.take(moved_x, received_at, axis=0)
    cell_rows = slab_x.reshape(-1, width)
    local_gram = lax.dot_general(cell_rows, cell_rows, contract, preferred_element_type=jnp.float32)
    gram_total, cross_total = lax.psum((local_gram, local_cross), ("space", "snap"))
    identity = jnp.eye(width, dtype=jnp.float32)
    lower = jnp.linalg.cholesky(gram_total / rows_total)
    inverse = lax.linalg.triangular_solve(lower, identity, left_side=True, lower=True)
    basis_rows = jnp.dot(cell_rows.astype(jnp.float32), inverse.T, precision=lax.Precision.HIGHEST)
    projection = jnp.dot(inverse, cross_total, precision=lax.Precision.HIGHEST) / math.sqrt(
        rows_total
    )
    return (basis_rows.reshape(slab_x.shape[0], slab_x.shape[1], width), lower.T, projection)


def solution(mesh):
    in_specs = (P("space", None, "snap"), P("space", None, "snap"), P("space"))
    out_specs = (P("space", "snap", None), P(), P())
    return jax.shard_map(body, mesh=mesh, in_specs=in_specs, out_specs=out_specs, check_vma=False)
```

profile of v0, /device:TPU:1, one launch (start us, length us, event | category | flops | bytes accessed | tf_op | source)
XLA Modules:
  0.0 512.9 jit_solution(7003955340530065894)
XLA Ops:
  8.4 8.6 %all-to-all-start = ((s32[32,1,128]{2,1,0:T(1,128)}), s32[32,1,128]{2,1,0:T(1,128)S(1)}, u32[]{:S(2)}, u32[]{:S(2)}) async-start(s32[32,1,128]{2,1,0:T(1,128)} %broadcast_in_dim.58), calls=%async_computation | async-start | bytes 32768 | tf_op jit(solution)/shard_map/all_to_all | solution.py:20
  17.0 6.9 %copy.48 = bf16[128,128,128]{2,0,1:T(8,128)(2,1)} copy(bf16[128,128,128]{2,1,0:T(8,128)(2,1)} %param.3) | data formatting | bytes 8388608 | tf_op args[0]
  23.9 5.0 all-to-all-start.1
  29.0 6.9 %copy.55 = bf16[128,128,128]{2,0,1:T(8,128)(2,1)} copy(bf16[128,128,128]{2,1,0:T(8,128)(2,1)} %param.4) | data formatting | bytes 8388608 | tf_op args[1]
  35.8 42.1 %all-to-all-done.1 = bf16[128,128,128]{2,0,1:T(8,128)(2,1)} async-done(((bf16[128,128,128]{2,0,1:T(8,128)(2,1)}), bf16[128,128,128]{2,0,1:T(8,128)(2,1)}, u32[]{:S(2)}, u32[]{:S(2)}) %all-to-all-start.1) | async-done | bytes 4194336 | tf_op jit(solution)/shard_map/all_to_all | solution.py:73
  84.0 6.4 %copy.50 = bf16[128,32,4,128]{0,3,2,1:T(8,128)(2,1)} copy(bf16[128,32,4,128]{3,0,1,2:T(8,128)(2,1)} %bitcast.6) | data formatting | bytes 8388608 | tf_op jit(solution)/shard_map/all_to_all | solution.py:73
  90.5 7.9 %copy.51 = bf16[128,32,512]{2,1,0:T(8,128)(2,1)} copy(bf16[128,32,512]{0,2,1:T(8,128)(2,1)} %bitcast.79) | data formatting | bytes 8388608 | tf_op jit(solution)/shard_map/all_to_all | solution.py:73
  98.4 5.0 gather_fusion.1
  108.0 22.3 %all-to-all-done.3 = bf16[128,128,128]{2,0,1:T(8,128)(2,1)} async-done(((bf16[128,128,128]{2,0,1:T(8,128)(2,1)}), bf16[128,128,128]{2,0,1:T(8,128)(2,1)}, u32[]{:S(2)}, u32[]{:S(2)}) %all-to-all-start.3) | async-done | bytes 4194336 | tf_op jit(solution)/shard_map/all_to_all | solution.py:74
  130.3 9.6 %all-to-all-start.2 = ((bf16[128,32,512]{2,1,0:T(8,128)(2,1)}), bf16[128,32,512]{2,1,0:T(8,128)(2,1)}, u32[]{:S(2)}, u32[]{:S(2)}) async-start(bf16[128,32,512]{2,1,0:T(8,128)(2,1)} %broadcast_select_fusion.1), calls=%async_computation.2 | async-start | bytes 8388608 | tf_op jit(solution)/shard_map/all_to_all | solution.py:85
  143.7 4.9 copy.49
  153.2 5.4 %copy.56 = bf16[128,4,32,128]{3,1,2,0:T(4,128)(2,1)S(1)} copy(bf16[128,4,32,128]{3,0,2,1:T(8,128)(2,1)} %bitcast.23) | data formatting | bytes 8388608 | tf_op jit(solution)/shard_map/all_to_all | solution.py:74
  162.1 28.4 %all-to-all-done.2 = bf16[128,32,512]{2,1,0:T(8,128)(2,1)} async-done(((bf16[128,32,512]{2,1,0:T(8,128)(2,1)}), bf16[128,32,512]{2,1,0:T(8,128)(2,1)}, u32[]{:S(2)}, u32[]{:S(2)}) %all-to-all-start.2) | async-done | bytes 4194336 | tf_op jit(solution)/shard_map/all_to_all | solution.py:85
  197.4 147.6 %all-reduce.4.cloned.1.call-done = (f32[512,512]{0,1:T(8,128)}, f32[512,512]{1,0:T(8,128)}) async-done(((f32[512,512]{0,1:T(8,128)}, f32[512,512]{1,0:T(8,128)}), (f32[512,512]{0,1:T(8,128)}, f32[512,512]{1,0:T(8,128)})) %all-reduce.4.cloned.1.call-update) | async-done | bytes 2097168 | tf_op jit(solution)/shard_map/psum | solution.py:91
  348.1 11.7 %cholesky.96 = f32[128,128]{1,0:T(8,128)S(1)} custom-call(f32[128,128]{1,0:T(8,128)S(1)} %cholesky.250), custom_call_target="Cholesky" | custom-call | tf_op jit(solution)/shard_map/jit(cholesky)/cholesky | solution.py:93
  359.8 9.8 %custom-call.30 = f32[1,128,128]{1,2,0:T(8,128)S(1)} custom-call(f32[1,128,128]{2,1,0:T(8,128)S(1)} %get-tuple-element.56), custom_call_target="InvertDiagBlocksLowerTriangular" | custom-call | tf_op jit(solution)/shard_map/jit(cholesky)/cholesky | solution.py:93
  372.4 11.9 %cholesky.201 = f32[128,128]{1,0:T(8,128)S(1)} custom-call(f32[128,128]{1,0:T(8,128)S(1)} %cholesky.254), custom_call_target="Cholesky" | custom-call | tf_op jit(solution)/shard_map/jit(cholesky)/cholesky | solution.py:93
  384.3 9.8 %custom-call.31 = f32[1,128,128]{1,2,0:T(8,128)S(1)} custom-call(f32[1,128,128]{2,1,0:T(8,128)S(1)} %get-tuple-element.53), custom_call_target="InvertDiagBlocksLowerTriangular" | custom-call | tf_op jit(solution)/shard_map/jit(cholesky)/cholesky | solution.py:93
  395.7 11.7 %cholesky.222 = f32[128,128]{1,0:T(8,128)S(1)} custom-call(f32[128,128]{1,0:T(8,128)S(1)} %cholesky.259), custom_call_target="Cholesky" | custom-call | tf_op jit(solution)/shard_map/jit(cholesky)/cholesky | solution.py:93
  408.1 9.8 %custom-call.32 = f32[1,128,128]{1,2,0:T(8,128)S(1)} custom-call(f32[1,128,128]{2,1,0:T(8,128)S(1)} %get-tuple-element.50), custom_call_target="InvertDiagBlocksLowerTriangular" | custom-call | tf_op jit(solution)/shard_map/jit(cholesky)/cholesky | solution.py:93
  419.4 11.9 %cholesky.239 = f32[128,128]{1,0:T(8,128)S(1)} custom-call(f32[128,128]{1,0:T(8,128)S(1)} %convolution_subtract_fusion.5), custom_call_target="Cholesky" | custom-call | tf_op jit(solution)/shard_map/jit(cholesky)/cholesky | solution.py:93
  436.4 13.9 %while.1 = (s32[]{:T(128)}, f32[512,512]{1,0:T(8,128)}, s32[4,2]{0,1:T(2,128)S(1)}, f32[4,128,128]{2,1,0:T(8,128)}, s32[]{:T(128)}) while((s32[]{:T(128)}, f32[512,512]{1,0:T(8,128)}, s32[4,2]{0,1:T(2,128)S(1)}, f32[4,128,128]{2,1,0:T(8,128)}, s32[]{:T(128)}) %tuple.41), condition=%wide.while_cond, body=%wide.while_body.sunk | while | flops 2 | bytes 132705 | solution.py:94
  450.3 40.1 %custom-call.33 = f32[4,128,128]{1,2,0:T(8,128)S(1)} custom-call(f32[4,128,128]{2,1,0:T(8,128)} %get-tuple-element.12), custom_call_target="InvertDiagBlocksLowerTriangular" | custom-call | tf_op jit(solution)/shard_map/triangular_solve | solution.py:94
  496.4 5.1 fusion.5
  (92 shorter events, 66.3 us)
Async XLA Ops:
  8.4 15.5 %all-to-all-start = ((s32[32,1,128]{2,1,0:T(1,128)}), s32[32,1,128]{2,1,0:T(1,128)S(1)}, u32[]{:S(2)}, u32[]{:S(2)}) async-start(s32[32,1,128]{2,1,0:T(1,128)} %broadcast_in_dim.58), calls=%async_computation | async-start | bytes 32768 | tf_op jit(solution)/shard_map/all_to_all | solution.py:20
  23.9 54.0 %all-to-all-start.1 = ((bf16[128,128,128]{2,0,1:T(8,128)(2,1)}), bf16[128,128,128]{2,0,1:T(8,128)(2,1)}, u32[]{:S(2)}, u32[]{:S(2)}) async-start(bf16[128,128,128]{2,0,1:T(8,128)(2,1)} %copy.48), calls=%async_computation.1 | async-start | bytes 8388608 | tf_op jit(solution)/shard_map/all_to_all | solution.py:73
  35.8 47.0 %copy-start.6 = (s32[128]{0:T(128)S(1)}, s32[128]{0:T(128)}, u32[]{:S(2)}) copy-start(s32[128]{0:T(128)} %param.5) | copy-start | bytes 1540
  77.9 52.4 %all-to-all-start.3 = ((bf16[128,128,128]{2,0,1:T(8,128)(2,1)}), bf16[128,128,128]{2,0,1:T(8,128)(2,1)}, u32[]{:S(2)}, u32[]{:S(2)}) async-start(bf16[128,128,128]{2,0,1:T(8,128)(2,1)} %copy.55), calls=%async_computation.3 | async-start | bytes 8388608 | tf_op jit(solution)/shard_map/all_to_all | solution.py:74
  130.3 60.3 %all-to-all-start.2 = ((bf16[128,32,512]{2,1,0:T(8,128)(2,1)}), bf16[128,32,512]{2,1,0:T(8,128)(2,1)}, u32[]{:S(2)}, u32[]{:S(2)}) async-start(bf16[128,32,512]{2,1,0:T(8,128)(2,1)} %broadcast_select_fusion.1), calls=%async_computation.2 | async-start | bytes 8388608 | tf_op jit(solution)/shard_map/all_to_all | solution.py:85
  139.9 205.2 %all-reduce.4.cloned.1.call-start = ((), (), s32[]{:S(2)}) async-start(), calls=%async_computation.4 | async-start | bytes 4194304 | tf_op jit(solution)/shard_map/psum | solution.py:91
  193.5 2.7 copy-start.3
  345.1 1.8 copy-start
  347.1 1.0 copy-start.2
  369.7 121.0 %copy-start.1 = (f32[512,512]{1,0:T(8,128)S(1)}, f32[512,512]{1,0:T(8,128)}, u32[]{:S(2)}) copy-start(f32[512,512]{1,0:T(8,128)} %fusion.18) | copy-start | bytes 3145732
  490.4 5.9 %copy-start.4 = (bf16[64,32,512]{2,1,0:T(8,128)(2,1)S(1)}, bf16[64,32,512]{2,1,0:T(8,128)(2,1)}, u32[]{:S(2)}) copy-start(bf16[64,32,512]{2,1,0:T(8,128)(2,1)} %copy-done.3) | copy-start | bytes 6291460
  495.9 5.5 %copy-start.5 = (f32[512,512]{1,0:T(8,128)S(1)}, f32[512,512]{1,0:T(8,128)}, u32[]{:S(2)}) copy-start(f32[512,512]{1,0:T(8,128)} %get-tuple-element.40) | copy-start | bytes 3145732
Sparse Core Ops, SparseCore 0:
  196.3 148.7 all-reduce.3
where the time goes:
time: 522 us; the launch traced here: 513 us
  waiting for transfers between devices  241 us (46%)
  other arithmetic  131 us (25%)
  local copies, waits for them, and re-layouts  70.2 us (13%)
  starting transfers between devices  28.1 us (5%)
  matrix products  25.5 us (5%)
  between operations  17.4 us (3%)
    psum x1, waiting for transfers between devices, body(): lax.psum((local_gram, local_cross), ('space', 'snap'))  148 us
    another operation x14, other arithmetic, body(): lower = jnp.linalg.cholesky(gram_total / rows_total)  78.8 us
    all_to_all x1, waiting for transfers between devices, body(): lax.all_to_all(owned_x, 'snap', split_axis=1, concat_axis=2, tiled=True)  42.1 us
    another operation x2, other arithmetic, body(): lax.linalg.triangular_solve(lower, identity, left_side=True, lower=True)  40.1 us
    all_to_all x1, waiting for transfers between devices, body(): lax.all_to_all(pick_rows(block_x, outgoing_table), 'space', split_axis=0,...  28.4 us
    all_to_all x1, waiting for transfers between devices, body(): lax.all_to_all(owned_y, 'snap', split_axis=1, concat_axis=2, tiled=True)  22.3 us
    all_to_all x3, local copies, waits for them, and re-layouts, body(): lax.all_to_all(owned_x, 'snap', split_axis=1, concat_axis=2, tiled=True)  19.3 us
    unnamed x17, local copies, waits for them, and re-layouts  16.1 us
  transfers between devices with their start and end apart: 5, of which 4 were waited for; matrix products, arithmetic and copies ran while one was open for 12% of the time, Pallas kernels for 0%

commit v1 on v0

--- a/solution.py
+++ b/solution.py
@@ -4,6 +4,106 @@
 import jax.numpy as jnp
 from jax import lax
 from jax.sharding import PartitionSpec as P
+
+
+from jax.experimental import pallas as pl
+from jax.experimental.pallas import tpu as pltpu
+HI = lax.Precision.HIGHEST
+
+def small_inv(P, b):
+    if b == 1:
+        return [[1.0 / P[0][0]]]
+    if b == 2:
+        a, h, d = P[0][0], P[0][1], P[1][1]
+        r = 1.0 / (a * d - h * h)
+        return [[d * r, -h * r], [-h * r, a * r]]
+    h = b // 2
+    A = [[P[i][j] for j in range(h)] for i in range(h)]
+    B = [[P[i][h + j] for j in range(h)] for i in range(h)]
+    D = [[P[h + i][h + j] for j in range(h)] for i in range(h)]
+    Ai = small_inv(A, h)
+    AiB = [[sum(Ai[i][k] * B[k][j] for k in range(h)) for j in range(h)] for i in range(h)]
+    S = [[None] * h for _ in range(h)]
+    for i in range(h):
+        for j in range(i, h):
+            S[i][j] = D[i][j] - sum(B[k][i] * AiB[k][j] for k in range(h))
+            S[j][i] = S[i][j]
+    Si = small_inv(S, h)
+    out = [[None] * b for _ in range(b)]
+    BS = [[sum(AiB[i][k] * Si[k][j] for k in range(h)) for j in range(h)] for i in range(h)]
+    for i in range(h):
+        for j in range(h):
+            out[h + i][h + j] = Si[i][j]
+            out[i][h + j] = -BS[i][j]
+            out[h + j][i] = -BS[i][j]
+    for i in range(h):
+        for j in range(i, h):
+            v = Ai[i][j] + sum(BS[i][k] * AiB[j][k] for k in range(h))
+            out[i][j] = v
+            out[j][i] = v
+    return out
+
+def diag_block(D, b, r_out, w_out):
+    lane = lax.broadcasted_iota(jnp.int32, (1, 128), 1)
+    sub = lax.broadcasted_iota(jnp.int32, (8, 1), 0)
+    M = list(D)
+    for g in range(0, 128, b):
+        v0, s0 = g // 8, g % 8
+        r = [M[v0][s0 + s:s0 + s + 1, :] for s in range(b)]
+        C0 = [jnp.broadcast_to(M[v0][:, g + t:g + t + 1], (8, 128)) for t in range(b)]
+        P = [[C0[t][s0 + s:s0 + s + 1, :] for t in range(b)] for s in range(b)]
+        ingroup = (lane >= g) & (lane < g + b)
+        rp = [jnp.where(ingroup, jnp.where(lane == g + s, 1.0, 0.0), r[s]) for s in range(b)]
+        if g + b < 128:
+            Pi = small_inv(P, b)
+            rt = [sum(Pi[s][t] * rp[t] for t in range(b)) for s in range(b)]
+            for v in range(v0, 16):
+                if v == v0 and s0 + b >= 8:
+                    continue
+                new = jnp.where(ingroup, 0.0, M[v])
+                for s in range(b):
+                    cs = C0[s] if v == v0 else M[v][:, g + s:g + s + 1]
+                    new = new - cs * rt[s]
+                if v == v0:
+                    new = jnp.where(sub >= s0 + b, new, M[v])
+                M[v] = new
+        er, eb = list(r), list(rp)
+        p = [list(row) for row in P]
+        for s in range(b):
+            sc = lax.rsqrt(p[s][s])
+            for t in range(s + 1, b):
+                m = p[s][t] / p[s][s]
+                er[t] = er[t] - m * er[s]
+                eb[t] = eb[t] - m * eb[s]
+                for q in range(t, b):
+                    p[t][q] = p[t][q] - m * p[s][q]
+            r_out[g + s:g + s + 1, :] = jnp.where(lane >= g + s, er[s] * sc, 0.0)
+            w_out[g + s:g + s + 1, :] = jnp.where(lane <= g + s, eb[s] * sc, 0.0)
+
+def factor(M, R, W, wk, rk, nblk=4, b=4):
+    n = nblk * 128
+    colb = lax.broadcasted_iota(jnp.int32, (1, n), 1) // 128
+    def outer(k, _):
+        o = pl.multiple_of(k * 128, 128)
+        kb = pl.ds(o, 128)
+        D = [M[pl.ds(pl.multiple_of(o + 8 * v, 8), 8), kb] for v in range(16)]
+        diag_block(D, b, rk, wk)
+        M[kb, kb] = (lax.broadcasted_iota(jnp.int32, (128, 128), 0) == lax.broadcasted_iota(jnp.int32, (128, 128), 1)).astype(jnp.float32)
+        row = jnp.dot(wk[...], M[kb, :], precision=HI, preferred_element_type=jnp.float32)
+        M[kb, :] = row
+        W[kb, :] = jnp.where(colb <= k, row, 0.0)
+        R[kb, :] = jnp.where(colb > k, row, 0.0)
+        R[kb, kb] = rk[...]
+        def trail(i, _):
+            ib = pl.ds(pl.multiple_of(i * 128, 128), 128)
+            lik = M[kb, ib]
+            upd = lax.dot_general(lik, M[kb, :], (((0,), (0,)), ((), ())), precision=HI, preferred_element_type=jnp.float32)
+            M[ib, :] = jnp.where(colb == k, 0.0, M[ib, :]) - upd
+            return 0
+        lax.fori_loop(k + 1, nblk, trail, 0)
+        return 0
+    lax.fori_loop(0, nblk, outer, 0)
+
 
 PATCH = 128
 BLK_DEV = 64
@@ -55,6 +155,24 @@
 
 def pick_rows(payload, indices):
     return jnp.take(payload, indices, axis=0, mode="fill", fill_value=0)
+
+
+def factor_kernel(g, R, W, M, wk, rk):
+    M[...] = g[...]
+    factor(M, R, W, wk, rk)
+
+
+def factor_call(g):
+    S = jax.ShapeDtypeStruct((512, 512), jnp.float32)
+    V = pl.BlockSpec(memory_space=pltpu.VMEM)
+    small = pltpu.VMEM((128, 128), jnp.float32)
+    return pl.pallas_call(
+        factor_kernel,
+        out_shape=(S, S),
+        in_specs=[V],
+        out_specs=(V, V),
+        scratch_shapes=[pltpu.VMEM((512, 512), jnp.float32), small, small],
+    )(g)
 
 
 def body(owned_x, owned_y, patch_dest):
@@ -89,14 +207,12 @@
     cell_rows = slab_x.reshape(-1, width)
     local_gram = lax.dot_general(cell_rows, cell_rows, contract, preferred_element_type=jnp.float32)
     gram_total, cross_total = lax.psum((local_gram, local_cross), ("space", "snap"))
-    identity = jnp.eye(width, dtype=jnp.float32)
-    lower = jnp.linalg.cholesky(gram_total / rows_total)
-    inverse = lax.linalg.triangular_solve(lower, identity, left_side=True, lower=True)
+    upper, inverse = factor_call(gram_total / rows_total)
     basis_rows = jnp.dot(cell_rows.astype(jnp.float32), inverse.T, precision=lax.Precision.HIGHEST)
     projection = jnp.dot(inverse, cross_total, precision=lax.Precision.HIGHEST) / math.sqrt(
         rows_total
     )
-    return (basis_rows.reshape(slab_x.shape[0], slab_x.shape[1], width), lower.T, projection)
+    return (basis_rows.reshape(slab_x.shape[0], slab_x.shape[1], width), upper, projection)
 
 
 def solution(mesh):

time: 522 us -> 391 us (0.75); the launches traced: 513 us -> 390 us
  other arithmetic: 131 us -> 10.1 us
  Pallas kernels: 0 us -> 26.7 us
  local copies, waits for them, and re-layouts: 70.2 us -> 53.6 us
  matrix products: 25.5 us -> 15.1 us
    another operation x16 -> x0, other arithmetic: 119 us -> none  [the longest x14 78.8 us: body(): lower = jnp.linalg.cholesky(gram_total / rows_total)]
    pallas_call x0 -> x1, Pallas kernels: none -> 26.7 us  [factor_call(): pl.pallas_call(factor_kernel, out_shape=(S, S), in_specs=[V], out_specs=(...]
    another operation x17 -> x0, local copies, waits for them, and re-layouts: 14 us -> none
    another operation x13 -> x0, matrix products: 11.4 us -> none  [the longest x7 5.86 us: body(): lax.linalg.triangular_solve(lower, identity, left_side=True, lower=True)]
    unnamed x17 -> x8, local copies, waits for them, and re-layouts: 16.1 us -> 13.8 us
  transfers between devices with their start and end apart: 5 -> 5, of which waited for: 4 -> 4; matrix products, arithmetic and copies ran while one was open for 12% -> 16% of each run, Pallas kernels for 0% -> 0%
where the time goes in v1:
time: 391 us; the launch traced here: 390 us
  waiting for transfers between devices  242 us (62%)
  local copies, waits for them, and re-layouts  53.6 us (14%)
  starting transfers between devices  28.1 us (7%)
  Pallas kernels  26.7 us (7%)
  matrix products  15.1 us (4%)
  between operations  14.2 us (4%)
  other arithmetic  10.1 us (3%)
    psum x1, waiting for transfers between devices, body(): lax.psum((local_gram, local_cross), ('space', 'snap'))  149 us
    all_to_all x1, waiting for transfers between devices, body(): lax.all_to_all(owned_x, 'snap', split_axis=1, concat_axis=2, tiled=True)  42.1 us
    all_to_all x1, waiting for transfers between devices, body(): lax.all_to_all(pick_rows(block_x, outgoing_table), 'space', split_axis=0,...  28.7 us
    pallas_call x1, Pallas kernels, factor_call(): pl.pallas_call(factor_kernel, out_shape=(S, S), in_specs=[V], out_specs=(...  26.7 us
    all_to_all x1, waiting for transfers between devices, body(): lax.all_to_all(owned_y, 'snap', split_axis=1, concat_axis=2, tiled=True)  22.3 us
    all_to_all x3, local copies, waits for them, and re-layouts, body(): lax.all_to_all(owned_x, 'snap', split_axis=1, concat_axis=2, tiled=True)  19.3 us
    unnamed x8, local copies, waits for them, and re-layouts  13.8 us
    all_to_all x1, starting transfers between devices, body(): lax.all_to_all(pick_rows(block_x, outgoing_table), 'space', split_axis=0,...  9.61 us
  transfers between devices with their start and end apart: 5, of which 4 were waited for; matrix products, arithmetic and copies ran while one was open for 16% of the time, Pallas kernels for 0%

profile of v1, /device:TPU:1, one launch (start us, length us, event | category | flops | bytes accessed | tf_op | source)
XLA Modules:
  0.0 389.8 jit_solution(14043044885130857175)
XLA Ops:
  8.4 8.6 %all-to-all-start = ((s32[32,1,128]{2,1,0:T(1,128)}), s32[32,1,128]{2,1,0:T(1,128)S(1)}, u32[]{:S(2)}, u32[]{:S(2)}) async-start(s32[32,1,128]{2,1,0:T(1,128)} %broadcast_in_dim.56), calls=%async_computation | async-start | bytes 32768 | tf_op jit(solution)/shard_map/all_to_all | solution.py:120
  17.0 6.9 %copy.33 = bf16[128,128,128]{2,0,1:T(8,128)(2,1)} copy(bf16[128,128,128]{2,1,0:T(8,128)(2,1)} %param.3) | data formatting | bytes 8388608 | tf_op args[0]
  23.9 5.0 %all-to-all-start.1 = ((bf16[128,128,128]{2,0,1:T(8,128)(2,1)}), bf16[128,128,128]{2,0,1:T(8,128)(2,1)}, u32[]{:S(2)}, u32[]{:S(2)}) async-start(bf16[128,128,128]{2,0,1:T(8,128)(2,1)} %copy.33), calls=%async_computation.1 | async-start | bytes 8388608 | tf_op jit(solution)/shard_map/all_to_all | solution.py:191
  29.0 6.9 %copy.38 = bf16[128,128,128]{2,0,1:T(8,128)(2,1)} copy(bf16[128,128,128]{2,1,0:T(8,128)(2,1)} %param.4) | data formatting | bytes 8388608 | tf_op args[1]
  35.8 42.1 %all-to-all-done.1 = bf16[128,128,128]{2,0,1:T(8,128)(2,1)} async-done(((bf16[128,128,128]{2,0,1:T(8,128)(2,1)}), bf16[128,128,128]{2,0,1:T(8,128)(2,1)}, u32[]{:S(2)}, u32[]{:S(2)}) %all-to-all-start.1) | async-done | bytes 4194336 | tf_op jit(solution)/shard_map/all_to_all | solution.py:191
  77.9 4.8 %all-to-all-start.3 = ((bf16[128,128,128]{2,0,1:T(8,128)(2,1)}), bf16[128,128,128]{2,0,1:T(8,128)(2,1)}, u32[]{:S(2)}, u32[]{:S(2)}) async-start(bf16[128,128,128]{2,0,1:T(8,128)(2,1)} %copy.38), calls=%async_computation.3 | async-start | bytes 8388608 | tf_op jit(solution)/shard_map/all_to_all | solution.py:192
  84.0 6.4 %copy.35 = bf16[128,32,4,128]{0,3,2,1:T(8,128)(2,1)} copy(bf16[128,32,4,128]{3,0,1,2:T(8,128)(2,1)} %bitcast.6) | data formatting | bytes 8388608 | tf_op jit(solution)/shard_map/all_to_all | solution.py:191
  90.5 7.9 %copy.36 = bf16[128,32,512]{2,1,0:T(8,128)(2,1)} copy(bf16[128,32,512]{0,2,1:T(8,128)(2,1)} %bitcast.31) | data formatting | bytes 8388608 | tf_op jit(solution)/shard_map/all_to_all | solution.py:191
  98.4 5.0 %gather_fusion.1 = bf16[128,32,512]{2,1,0:T(8,128)(2,1)} fusion(bf16[128,32,512]{2,1,0:T(8,128)(2,1)} %copy.36, s32[1024]{0:T(1024)S(1)} %pad_clamp_fusion.1), kind=kCustom, calls=%fused_computation.1 | custom fusion | bytes 8389120 | tf_op jit(solution)/shard_map/jit(_take)/gather | solution.py:157
  103.4 4.6 %broadcast_select_fusion.1 = bf16[128,32,512]{2,1,0:T(8,128)(2,1)} fusion(bf16[128,32,512]{2,1,0:T(8,128)(2,1)} %gather_fusion.1, pred[128]{0:T(512)(128)(4,1)S(1)} %compare_and_fusion), kind=kLoop, calls=%fused_computation.10 | loop fusion | flops 2097152 | bytes 8388736 | tf_op jit(solution)/shard_map/jit(_take)/select_n | solution.py:157
  108.0 22.3 %all-to-all-done.3 = bf16[128,128,128]{2,0,1:T(8,128)(2,1)} async-done(((bf16[128,128,128]{2,0,1:T(8,128)(2,1)}), bf16[128,128,128]{2,0,1:T(8,128)(2,1)}, u32[]{:S(2)}, u32[]{:S(2)}) %all-to-all-start.3) | async-done | bytes 4194336 | tf_op jit(solution)/shard_map/all_to_all | solution.py:192
  130.3 9.6 %all-to-all-start.2 = ((bf16[128,32,512]{2,1,0:T(8,128)(2,1)}), bf16[128,32,512]{2,1,0:T(8,128)(2,1)}, u32[]{:S(2)}, u32[]{:S(2)}) async-start(bf16[128,32,512]{2,1,0:T(8,128)(2,1)} %broadcast_select_fusion.1), calls=%async_computation.2 | async-start | bytes 8388608 | tf_op jit(solution)/shard_map/all_to_all | solution.py:203
  143.4 4.9 %copy.34 = bf16[128,128,128]{2,1,0:T(8,128)(2,1)S(1)} copy(bf16[128,128,128]{2,0,1:T(8,128)(2,1)} %all-to-all-done.1) | data formatting | bytes 8388608 | tf_op jit(solution)/shard_map/all_to_all | solution.py:191
  148.7 4.2 %copy.37 = bf16[128,32,4,128]{3,2,1,0:T(4,128)(2,1)S(1)} copy(bf16[128,32,4,128]{3,1,2,0:T(8,128)(2,1)S(1)} %broadcast_select_fusion) | data formatting | bytes 8388608 | tf_op jit(solution)/shard_map/jit(_where)/select_n | solution.py:196
  152.9 5.4 %copy.39 = bf16[128,4,32,128]{3,1,2,0:T(4,128)(2,1)S(1)} copy(bf16[128,4,32,128]{3,0,2,1:T(8,128)(2,1)} %bitcast.11) | data formatting | bytes 8388608 | tf_op jit(solution)/shard_map/all_to_all | solution.py:192
  158.3 3.6 fusion
  161.9 28.7 %all-to-all-done.2 = bf16[128,32,512]{2,1,0:T(8,128)(2,1)} async-done(((bf16[128,32,512]{2,1,0:T(8,128)(2,1)}), bf16[128,32,512]{2,1,0:T(8,128)(2,1)}, u32[]{:S(2)}, u32[]{:S(2)}) %all-to-all-start.2) | async-done | bytes 4194336 | tf_op jit(solution)/shard_map/all_to_all | solution.py:203
  190.6 2.9 gather_fusion.2
  193.5 2.4 convolution_bitcast_fusion
  195.9 148.8 %all-reduce.3.cloned.1.call-done = (f32[512,512]{1,0:T(8,128)}, f32[512,512]{1,0:T(8,128)}) async-done(((f32[512,512]{1,0:T(8,128)}, f32[512,512]{1,0:T(8,128)}), (f32[512,512]{1,0:T(8,128)}, f32[512,512]{1,0:T(8,128)})) %all-reduce.3.cloned.1.call-update) | async-done | bytes 2097168 | tf_op jit(solution)/shard_map/psum | solution.py:209
  344.7 2.3 broadcast_multiply_fusion.g
  347.0 26.7 %shard_map.58 = (f32[512,512]{1,0:T(8,128)}, f32[512,512]{1,0:T(8,128)}) custom-call(f32[512,512]{1,0:T(8,128)} %broadcast_multiply_fusion.g), custom_call_target="tpu_custom_call" | custom-call | tf_op jit(solution)/shard_map/pallas_call | solution.py:169
  373.7 6.4 %fusion.5 = f32[64,32,512]{2,1,0:T(8,128)} fusion(f32[512,512]{1,0:T(8,128)} %get-tuple-element.7, bf16[64,32,512]{2,1,0:T(8,128)(2,1)S(1)} %gather_fusion.2, pred[64]{0:T(512)(128)(4,1)S(1)} %get-tuple-element.11), kind=kOutput, calls=%fused_computation.15 | convolution fusion | flops 6443499520 | bytes 7340096 | tf_op jit(solution)/shard_map/dot_general | solution.py:211
  380.1 2.8 convolution_multiply_fusion
  (31 shorter events, 6.3 us)
Async XLA Ops:
  8.4 15.5 %all-to-all-start = ((s32[32,1,128]{2,1,0:T(1,128)}), s32[32,1,128]{2,1,0:T(1,128)S(1)}, u32[]{:S(2)}, u32[]{:S(2)}) async-start(s32[32,1,128]{2,1,0:T(1,128)} %broadcast_in_dim.56), calls=%async_computation | async-start | bytes 32768 | tf_op jit(solution)/shard_map/all_to_all | solution.py:120
  23.9 54.0 %all-to-all-start.1 = ((bf16[128,128,128]{2,0,1:T(8,128)(2,1)}), bf16[128,128,128]{2,0,1:T(8,128)(2,1)}, u32[]{:S(2)}, u32[]{:S(2)}) async-start(bf16[128,128,128]{2,0,1:T(8,128)(2,1)} %copy.33), calls=%async_computation.1 | async-start | bytes 8388608 | tf_op jit(solution)/shard_map/all_to_all | solution.py:191
  35.8 47.0 %copy-start.2 = (s32[128]{0:T(128)S(1)}, s32[128]{0:T(128)}, u32[]{:S(2)}) copy-start(s32[128]{0:T(128)} %param.5) | copy-start | bytes 1540
  77.9 52.4 %all-to-all-start.3 = ((bf16[128,128,128]{2,0,1:T(8,128)(2,1)}), bf16[128,128,128]{2,0,1:T(8,128)(2,1)}, u32[]{:S(2)}, u32[]{:S(2)}) async-start(bf16[128,128,128]{2,0,1:T(8,128)(2,1)} %copy.38), calls=%async_computation.3 | async-start | bytes 8388608 | tf_op jit(solution)/shard_map/all_to_all | solution.py:192
  130.3 60.3 %all-to-all-start.2 = ((bf16[128,32,512]{2,1,0:T(8,128)(2,1)}), bf16[128,32,512]{2,1,0:T(8,128)(2,1)}, u32[]{:S(2)}, u32[]{:S(2)}) async-start(bf16[128,32,512]{2,1,0:T(8,128)(2,1)} %broadcast_select_fusion.1), calls=%async_computation.2 | async-start | bytes 8388608 | tf_op jit(solution)/shard_map/all_to_all | solution.py:203
  139.9 204.8 %all-reduce.3.cloned.1.call-start = ((), (), s32[]{:S(2)}) async-start(), calls=%async_computation.4 | async-start | bytes 4194304 | tf_op jit(solution)/shard_map/psum | solution.py:209
  347.0 33.1 %copy-start.1 = (f32[512,512]{1,0:T(8,128)S(1)}, f32[512,512]{1,0:T(8,128)}, u32[]{:S(2)}) copy-start(f32[512,512]{1,0:T(8,128)} %get-tuple-element.10) | copy-start | bytes 3145732
  373.7 6.4 %copy-start = (f32[512,512]{1,0:T(8,128)S(1)}, f32[512,512]{1,0:T(8,128)}, u32[]{:S(2)}) copy-start(f32[512,512]{1,0:T(8,128)} %get-tuple-element.7) | copy-start | bytes 3145732
Sparse Core Ops, SparseCore 0:
  196.0 148.6 all-reduce.2

commit v2 on v1

v2 whole, which is shorter than its diff:
```python
import jax
import jax.numpy as jnp
from jax import lax
from jax.experimental import pallas as pl
from jax.experimental.pallas import tpu as pltpu
from jax.sharding import PartitionSpec as P

BLK_DEV = 64
HI = lax.Precision.HIGHEST

def small_inv(P, b):
    if b == 1:
        return [[1.0 / P[0][0]]]
    if b == 2:
        a, h, d = P[0][0], P[0][1], P[1][1]
        r = 1.0 / (a * d - h * h)
        return [[d * r, -h * r], [-h * r, a * r]]
    h = b // 2
    A = [[P[i][j] for j in range(h)] for i in range(h)]
    B = [[P[i][h + j] for j in range(h)] for i in range(h)]
    D = [[P[h + i][h + j] for j in range(h)] for i in range(h)]
    Ai = small_inv(A, h)
    AiB = [[sum(Ai[i][k] * B[k][j] for k in range(h)) for j in range(h)] for i in range(h)]
    S = [[None] * h for _ in range(h)]
    for i in range(h):
        for j in range(i, h):
            S[i][j] = D[i][j] - sum(B[k][i] * AiB[k][j] for k in range(h))
            S[j][i] = S[i][j]
    Si = small_inv(S, h)
    out = [[None] * b for _ in range(b)]
    BS = [[sum(AiB[i][k] * Si[k][j] for k in range(h)) for j in range(h)] for i in range(h)]
    for i in range(h):
        for j in range(h):
            out[h + i][h + j] = Si[i][j]
            out[i][h + j] = -BS[i][j]
            out[h + j][i] = -BS[i][j]
    for i in range(h):
        for j in range(i, h):
            v = Ai[i][j] + sum(BS[i][k] * AiB[j][k] for k in range(h))
            out[i][j] = v
            out[j][i] = v
    return out

def diag_block(D, b, r_out, w_out):
    lane = lax.broadcasted_iota(jnp.int32, (1, 128), 1)
    sub = lax.broadcasted_iota(jnp.int32, (8, 1), 0)
    M = list(D)
    for g in range(0, 128, b):
        v0, s0 = g // 8, g % 8
        r = [M[v0][s0 + s:s0 + s + 1, :] for s in range(b)]
        C0 = [jnp.broadcast_to(M[v0][:, g + t:g + t + 1], (8, 128)) for t in range(b)]
        P = [[C0[t][s0 + s:s0 + s + 1, :] for t in range(b)] for s in range(b)]
        ingroup = (lane >= g) & (lane < g + b)
        rp = [jnp.where(ingroup, jnp.where(lane == g + s, 1.0, 0.0), r[s]) for s in range(b)]
        if g + b < 128:
            Pi = small_inv(P, b)
            rt = [sum(Pi[s][t] * rp[t] for t in range(b)) for s in range(b)]
            for v in range(v0, 16):
                if v == v0 and s0 + b >= 8:
                    continue
                new = jnp.where(ingroup, 0.0, M[v])
                for s in range(b):
                    cs = C0[s] if v == v0 else M[v][:, g + s:g + s + 1]
                    new = new - cs * rt[s]
                if v == v0:
                    new = jnp.where(sub >= s0 + b, new, M[v])
                M[v] = new
        er, eb = list(r), list(rp)
        p = [list(row) for row in P]
        for s in range(b):
            sc = lax.rsqrt(p[s][s])
            for t in range(s + 1, b):
                m = p[s][t] / p[s][s]
                er[t] = er[t] - m * er[s]
                eb[t] = eb[t] - m * eb[s]
                for q in range(t, b):
                    p[t][q] = p[t][q] - m * p[s][q]
            r_out[g + s:g + s + 1, :] = jnp.where(lane >= g + s, er[s] * sc, 0.0)
            w_out[g + s:g + s + 1, :] = jnp.where(lane <= g + s, eb[s] * sc, 0.0)

def factor(M, R, W, wk, rk, nblk=4, b=4):
    n = nblk * 128
    colb = lax.broadcasted_iota(jnp.int32, (1, n), 1) // 128
    def outer(k, _):
        o = pl.multiple_of(k * 128, 128)
        kb = pl.ds(o, 128)
        D = [M[pl.ds(pl.multiple_of(o + 8 * v, 8), 8), kb] for v in range(16)]
        diag_block(D, b, rk, wk)
        M[kb, kb] = (lax.broadcasted_iota(jnp.int32, (128, 128), 0) == lax.broadcasted_iota(jnp.int32, (128, 128), 1)).astype(jnp.float32)
        row = jnp.dot(wk[...], M[kb, :], precision=HI, preferred_element_type=jnp.float32)
        M[kb, :] = row
        W[kb, :] = jnp.where(colb <= k, row, 0.0)
        R[kb, :] = jnp.where(colb > k, row, 0.0)
        R[kb, kb] = rk[...]
        def trail(i, _):
            ib = pl.ds(pl.multiple_of(i * 128, 128), 128)
            lik = M[kb, ib]
            upd = lax.dot_general(lik, M[kb, :], (((0,), (0,)), ((), ())), precision=HI, preferred_element_type=jnp.float32)
            M[ib, :] = jnp.where(colb == k, 0.0, M[ib, :]) - upd
            return 0
        lax.fori_loop(k + 1, nblk, trail, 0)
        return 0
    lax.fori_loop(0, nblk, outer, 0)


ROWS = 262144
MESH = pl.DeviceIdType.MESH
F32 = jnp.float32
BF16 = jnp.bfloat16
ORDER = (0, 2, 1, 3)
CHUNKS = 8
GT = 160
CT = 256


def where_am_i():
    s = lax.axis_index("space")
    return s // 8, (s // 2) % 4, s % 2, lax.axis_index("snap"), s


def space_of(y, x, c):
    return (lax.rem(y, 4) * 4 + lax.rem(x, 4)) * 2 + lax.rem(c, 2)


def remote(src, dst, ss, rs, space=None, snap=None):
    dev = {}
    if space is not None:
        dev["space"] = space
    if snap is not None:
        dev["snap"] = snap
    return pltpu.make_async_remote_copy(
        src_ref=src, dst_ref=dst, send_sem=ss, recv_sem=rs, device_id=dev, device_id_type=MESH
    )


def loop(lo, hi, body):
    def step(i, carry):
        body(i)
        return carry

    lax.fori_loop(lo, hi, step, 0)


def column(row):
    eye = lax.broadcasted_iota(jnp.int32, (128, 128), 0) == lax.broadcasted_iota(jnp.int32, (128, 128), 1)
    return jnp.sum(jnp.where(eye, jnp.broadcast_to(row, (128, 128)), 0), axis=1, keepdims=True)


def slot_tables(dest, y, x, c):
    slab = jnp.where(dest >= 0, dest // BLK_DEV, -1)
    lane = lax.broadcasted_iota(jnp.int32, (128, 128), 1)
    sub = lax.broadcasted_iota(jnp.int32, (128, 128), 0)
    same = (column(slab) == slab) & (sub < lane)
    rank = jnp.sum(same.astype(jnp.int32), axis=0, keepdims=True)
    dy = (slab // 8 - y + 4) % 4
    dx = ((slab // 2) % 4 - x + 4) % 4
    dc = (slab % 2 - c + 2) % 2
    place = jnp.where(dy == 1, 2, jnp.where(dy == 2, 1, dy))
    pos = ((dc * 4 + (dx - dy + 4) % 4) * 4 + place) * 4 + rank
    pos = column(jnp.where(dest >= 0, pos, -1))
    hit = pos == lane
    slot = jnp.sum(jnp.where(hit, sub - 128, 0), axis=0, keepdims=True) + 128
    block = jnp.sum(jnp.where(hit, column(dest) + 1, 0), axis=0, keepdims=True) - 1
    return slot, block


def all_sum(n, tiles, b1, half, b2, piece, zb, half2, full, s1, r1, s2, r2, s3, r3, s4, r4, s5, r5, after_z=None):
    y, x, c, z, s = where_am_i()
    chip = s // 2
    h, m = n // 2, n // 32
    mate = chip * 2 + (1 - c)
    cp1 = remote(tiles.at[pl.ds((1 - c) * h, h)], b1, s1.at[0], r1.at[0], space=mate)
    cp1.start()
    cp1.wait_recv()
    half[...] = tiles[pl.ds(c * h, h)] + b1[...]

    def chip_at(d):
        return lax.rem(y + d // 4, 4) * 4 + lax.rem(x + lax.rem(d, 4), 4)

    def scatter(d):
        q = chip_at(d)
        return remote(half.at[pl.ds(q * m, m)], b2.at[chip], s2.at[d], r2.at[d], space=q * 2 + c)

    loop(1, 16, lambda d: scatter(d).start())
    b2[chip] = half[pl.ds(chip * m, m)]
    loop(1, 16, lambda d: scatter(d).wait_recv())
    total = b2[0]
    for q in range(1, 16):
        total = total + b2[q]
    piece[...] = total
    zcp = [remote(piece, zb.at[z], s3.at[d - 1], r3.at[d - 1], snap=lax.rem(z + d, 4)) for d in (1, 2, 3)]
    for cp in zcp:
        cp.start()
    if after_z is not None:
        after_z()
    zb[z] = piece[...]
    for cp in zcp:
        cp.wait_recv()
    half2[pl.ds(chip * m, m)] = zb[0] + zb[1] + zb[2] + zb[3]

    def gather(d):
        mine = pl.ds(chip * m, m)
        return remote(half2.at[mine], half2.at[mine], s4.at[d], r4.at[d], space=chip_at(d) * 2 + c)

    loop(1, 16, lambda d: gather(d).start())
    loop(1, 16, lambda d: gather(d).wait_recv())
    cp5 = remote(half2, full.at[pl.ds(c * h, h)], s5.at[0], r5.at[0], space=mate)
    cp5.start()
    full[pl.ds(c * h, h)] = half2[...]
    cp5.wait_recv()

    def drain():
        cp1.wait_send()
        loop(1, 16, lambda d: scatter(d).wait_send())
        for cp in zcp:
            cp.wait_send()
        loop(1, 16, lambda d: gather(d).wait_send())
        cp5.wait_send()

    return drain


def sum_scratch(n):
    h, m = n // 2, n // 32
    dma = pltpu.SemaphoreType.DMA
    return [
        pltpu.VMEM((n, 8, 128), F32),
        pltpu.VMEM((h, 8, 128), F32),
        pltpu.VMEM((h, 8, 128), F32),
        pltpu.VMEM((16, m, 8, 128), F32),
        pltpu.VMEM((m, 8, 128), F32),
        pltpu.VMEM((4, m, 8, 128), F32),
        pltpu.VMEM((h, 8, 128), F32),
        pltpu.VMEM((n, 8, 128), F32),
        dma((1,)), dma((1,)), dma((16,)), dma((16,)), dma((3,)), dma((3,)), dma((16,)), dma((16,)), dma((1,)), dma((1,)),
    ]


def whole(dest, x_hbm, y_hbm, q_hbm, r_out, p_out, xin, yin, xo, yo, xr, yr, sr, xs, qv, acc, M, W, wk, rk,
          ids, tab_v, tab_s, at_v, at_s, lsem, tsem, qsem, xs_s, xs_r, ys_s, ys_r, sp_s, sp_r, id_s, id_r, *sums):
    y, x, c, z, s = where_am_i()
    gsum, csum = sums[:18], sums[18:]
    load_x = pltpu.make_async_copy(x_hbm, xin.at[pl.ds(0, 128)], lsem.at[0])
    load_y = pltpu.make_async_copy(y_hbm, yin.at[pl.ds(0, 128)], lsem.at[1])
    load_x.start()
    load_y.start()

    def space_at(k, j):
        a = ORDER[j]
        return space_of(y + a, x + a + lax.rem(k, 4), c + k // 4)

    barrier = pltpu.get_barrier_semaphore()
    for o in range(1, 32):
        pl.semaphore_signal(barrier, inc=1, device_id={"space": space_at(o // 4, o % 4)}, device_id_type=MESH)
    for d in (1, 2, 3):
        pl.semaphore_signal(barrier, inc=1, device_id={"snap": lax.rem(z + d, 4)}, device_id_type=MESH)

    xin[128] = jnp.zeros((128, 128), BF16)
    yin[128] = jnp.zeros((128, 128), BF16)
    slot, block = slot_tables(dest[...], y, x, c)
    tab_v[...] = jnp.broadcast_to(jnp.clip(slot, 0, 128), (8, 128))
    ids[s] = jnp.broadcast_to(block, (8, 128))
    tab_copy = pltpu.make_async_copy(tab_v, tab_s, tsem.at[0])
    tab_copy.start()
    tab_copy.wait()
    load_x.wait()

    def order_slots(src, dst, recv, k):
        def one(i):
            got = src[tab_s[0, i]]
            for q in range(4):
                dst[q, i] = got[32 * q:32 * q + 32]
            recv[z, i] = dst[z, i]

        loop(16 * k, 16 * k + 16, one)

    def over_z(src, recv, ss, rs, k):
        span = pl.ds(16 * k, 16)
        out = []
        for d in (1, 2, 3):
            to = lax.rem(z + d, 4)
            out.append(remote(src.at[to, span], recv.at[z, span], ss.at[k, d - 1], rs.at[k, d - 1], snap=to))
        return out

    def send_z(src, recv, ss, rs, k):
        for cp in over_z(src, recv, ss, rs, k):
            cp.start()

    order_slots(xin, xo, xr, 0)
    pl.semaphore_wait(barrier, 34)
    for k in range(1, CHUNKS):
        order_slots(xin, xo, xr, k)
        send_z(xo, xr, xs_s, xs_r, k - 1)
    load_y.wait()
    order_slots(yin, yo, yr, 0)
    send_z(xo, xr, xs_s, xs_r, CHUNKS - 1)

    def send_ids(k, j):
        o = 4 * k + j
        return remote(ids.at[s], ids.at[s], id_s.at[o], id_r.at[o], space=space_at(k, j))

    for o in range(1, 32):
        send_ids(o // 4, o % 4).start()
    loop(1, CHUNKS, lambda k: order_slots(yin, yo, yr, k))
    send_z(yo, yr, ys_s, ys_r, 0)

    for o in range(1, 32):
        send_ids(o // 4, o % 4).wait_recv()
    wanted = s * BLK_DEV + lax.broadcasted_iota(jnp.int32, (BLK_DEV, 1), 0)
    place = lax.rem(lax.broadcasted_iota(jnp.int32, (1, 128), 1), 4)
    found = jnp.zeros((BLK_DEV, 128), jnp.int32)
    for src in range(32):
        found = found + jnp.where(ids[src][0:1, :] == wanted, place + 4 * src, 0)
    found = jnp.sum(found, axis=1, keepdims=True)
    pick = lax.broadcasted_iota(jnp.int32, (BLK_DEV, 128), 0) == lax.broadcasted_iota(jnp.int32, (BLK_DEV, 128), 1)
    found = jnp.sum(jnp.where(pick, found, 0), axis=0, keepdims=True)
    at_v[...] = jnp.broadcast_to(jnp.clip(found, 0, 127), (8, 128))
    at_copy = pltpu.make_async_copy(at_v, at_s, tsem.at[1])
    at_copy.start()
    at_copy.wait()

    def to_slab(k, j):
        o = 4 * k + j
        return remote(xr.at[:, pl.ds(4 * o, 4)], sr.at[:, pl.ds(4 * s, 4)], sp_s.at[o], sp_r.at[o], space=space_at(k, j))

    def panel_rows(buf, k):
        return jnp.concatenate([buf[p, pl.ds(16 * k, 16)].reshape(512, 128) for p in range(4)], axis=1)

    acc[...] = jnp.zeros((512, 512), F32)
    contract = (((0,), (0,)), ((), ()))

    def gram_step(k):
        for cp in over_z(xo, xr, xs_s, xs_r, k):
            cp.wait_recv()
        for j in range(4):
            if j == 0:
                @pl.when(k > 0)
                def _():
                    to_slab(k, 0).start()

                @pl.when(k == 0)
                def _():
                    sr[:, pl.ds(4 * s, 4)] = xr[:, 0:4]
            else:
                to_slab(k, j).start()
        rows = panel_rows(xr, k)
        acc[...] += lax.dot_general(rows, rows, contract, preferred_element_type=F32)

    loop(0, CHUNKS, gram_step)

    def later_y():
        for k in range(1, CHUNKS):
            send_z(yo, yr, ys_s, ys_r, k)

    b = 0
    for i in range(4):
        for j in range(i, 4):
            gsum[0][16 * b:16 * b + 16] = acc[128 * i:128 * i + 128, 128 * j:128 * j + 128].reshape(16, 8, 128)
            b += 1
    drain_g = all_sum(GT, *gsum, after_z=later_y)
    full = gsum[7]
    b = 0
    for i in range(4):
        for j in range(i, 4):
            M[128 * i:128 * i + 128, 128 * j:128 * j + 128] = full[16 * b:16 * b + 16].reshape(128, 128) * (1.0 / ROWS)
            b += 1
    factor(M, r_out, W, wk, rk)

    for o in range(1, 32):
        to_slab(o // 4, o % 4).wait_recv()

    def pick_block(i):
        at = at_s[0, i]
        for p in range(4):
            xs[i, :, 128 * p:128 * p + 128] = sr[p, at]

    loop(0, BLK_DEV, pick_block)
    w1 = W[...].astype(BF16)
    w2 = (W[...] - w1.astype(F32)).astype(BF16)
    w3 = (W[...] - w1.astype(F32) - w2.astype(F32)).astype(BF16)
    last = (((1,), (1,)), ((), ()))

    def store_q(i):
        span = pl.ds(16 * i, 16)
        return pltpu.make_async_copy(qv.at[span], q_hbm.at[span], qsem.at[i])

    def basis(i):
        span = pl.ds(16 * i, 16)
        rows = xs[span].reshape(512, 512)
        out = lax.dot_general(rows, w3, last, preferred_element_type=F32)
        out = out + lax.dot_general(rows, w2, last, preferred_element_type=F32)
        out = out + lax.dot_general(rows, w1, last, preferred_element_type=F32)
        qv[span] = out.reshape(16, 32, 512)
        store_q(i).start()

    loop(0, 4, basis)

    acc[...] = jnp.zeros((512, 512), F32)

    def cross_step(k):
        for cp in over_z(yo, yr, ys_s, ys_r, k):
            cp.wait_recv()
        acc[...] += lax.dot_general(panel_rows(xr, k), panel_rows(yr, k), contract, preferred_element_type=F32)

    loop(0, CHUNKS, cross_step)
    for j in range(4):
        csum[0][64 * j:64 * j + 64] = acc[:, 128 * j:128 * j + 128].reshape(64, 8, 128)
    drain_c = all_sum(CT, *csum)
    for j in range(4):
        M[:, 128 * j:128 * j + 128] = csum[7][64 * j:64 * j + 64].reshape(512, 128)
    p_out[...] = jnp.dot(W[...], M[...], precision=HI, preferred_element_type=F32) * (1.0 / 512.0)

    loop(0, 4, lambda i: store_q(i).wait())
    drain_g()
    drain_c()
    for o in range(1, 32):
        send_ids(o // 4, o % 4).wait_send()
        to_slab(o // 4, o % 4).wait_send()

    def drain_z(k):
        for cp in over_z(xo, xr, xs_s, xs_r, k) + over_z(yo, yr, ys_s, ys_r, k):
            cp.wait_send()

    loop(0, CHUNKS, drain_z)


def body(owned_x, owned_y, patch_dest):
    V = pl.BlockSpec(memory_space=pltpu.VMEM)
    A = pl.BlockSpec(memory_space=pl.ANY)
    dma = pltpu.SemaphoreType.DMA
    square = jax.ShapeDtypeStruct((512, 512), F32)
    panels = pltpu.VMEM((4, 128, 32, 128), BF16)
    return pl.pallas_call(
        whole,
        out_shape=(jax.ShapeDtypeStruct((BLK_DEV, 32, 512), F32), square, square),
        in_specs=[V, A, A],
        out_specs=(A, V, V),
        scratch_shapes=[
            pltpu.VMEM((129, 128, 128), BF16),
            pltpu.VMEM((129, 128, 128), BF16),
            panels, panels, panels, panels, panels,
            pltpu.VMEM((BLK_DEV, 32, 512), BF16),
            pltpu.VMEM((BLK_DEV, 32, 512), F32),
            pltpu.VMEM((512, 512), F32),
            pltpu.VMEM((512, 512), F32),
            pltpu.VMEM((512, 512), F32),
            pltpu.VMEM((128, 128), F32),
            pltpu.VMEM((128, 128), F32),
            pltpu.VMEM((32, 8, 128), jnp.int32),
            pltpu.VMEM((8, 128), jnp.int32),
            pltpu.SMEM((8, 128), jnp.int32),
            pltpu.VMEM((8, 128), jnp.int32),
            pltpu.SMEM((8, 128), jnp.int32),
            dma((2,)), dma((2,)), dma((4,)),
            dma((CHUNKS, 3)), dma((CHUNKS, 3)), dma((CHUNKS, 3)), dma((CHUNKS, 3)),
            dma((32,)), dma((32,)), dma((32,)), dma((32,)),
        ] + sum_scratch(GT) + sum_scratch(CT),
        compiler_params=pltpu.CompilerParams(
            collective_id=0, has_side_effects=True, vmem_limit_bytes=63 << 20
        ),
        name="window",
    )(patch_dest.reshape(1, 128), owned_x, owned_y)


def solution(mesh):
    in_specs = (P("space", None, "snap"), P("space", None, "snap"), P("space"))
    out_specs = (P("space", "snap", None), P(), P())
    return jax.shard_map(body, mesh=mesh, in_specs=in_specs, out_specs=out_specs, check_vma=False)
```

time: 391 us -> 154 us (0.39)
  waiting for transfers between devices: 242 us -> 0 us
  Pallas kernels: 26.7 us -> 147 us
  local copies, waits for them, and re-layouts: 53.6 us -> 7.1 us
  starting transfers between devices: 28.1 us -> 0 us
  matrix products: 15.1 us -> 0 us
  between operations: 14.2 us -> 0.66 us
  other arithmetic: 10.1 us -> 0 us
    psum x1 -> x0, waiting for transfers between devices: 149 us -> none  [body(): lax.psum((local_gram, local_cross), ('space', 'snap'))]
    pallas_call x1, Pallas kernels: 26.7 us -> 147 us  [body(): pl.pallas_call(whole, out_shape=(jax.ShapeDtypeStruct((BLK_DEV, 32, 512),...]
    all_to_all x4 -> x0, waiting for transfers between devices: 93.1 us -> none  [the longest x1 42.1 us: body(): lax.all_to_all(owned_x, 'snap', split_axis=1, concat_axis=2, tiled=True)]
    all_to_all x4 -> x0, starting transfers between devices: 28.1 us -> none  [the longest x1 9.61 us: body(): lax.all_to_all(pick_rows(block_x, outgoing_table), 'space', split_axis=0,...]
    all_to_all x4 -> x0, local copies, waits for them, and re-layouts: 24.7 us -> none  [the longest x3 19.3 us: body(): lax.all_to_all(owned_x, 'snap', split_axis=1, concat_axis=2, tiled=True)]
    dot_general x4 -> x0, matrix products: 15.1 us -> none  [the longest x1 6.38 us: body(): jnp.dot(cell_rows.astype(jnp.float32), inverse.T, precision=lax.Precision...]
    gather x3 -> x0, local copies, waits for them, and re-layouts: 8.66 us -> none  [the longest x1 5.01 us: pick_rows(): return jnp.take(payload, indices, axis=0, mode='fill', fill_value=0)]
    unnamed x8 -> x7, local copies, waits for them, and re-layouts: 13.8 us -> 7.1 us
  transfers between devices with their start and end apart: 5 -> 0, of which waited for: 4 -> 0; matrix products, arithmetic and copies ran while one was open for 16% -> 0% of each run, Pallas kernels for 0% -> 0%
where the time goes in v2:
time: 154 us
  Pallas kernels  147 us (95%)
  local copies, waits for them, and re-layouts  7.1 us (5%)
    pallas_call x1, Pallas kernels, body(): pl.pallas_call(whole, out_shape=(jax.ShapeDtypeStruct((BLK_DEV, 32, 512),...  147 us
    unnamed x7, local copies, waits for them, and re-layouts  7.1 us

profile of v2, /device:TPU:1, one launch (start us, length us, event | category | flops | bytes accessed | tf_op | source)
XLA Modules:
  0.0 154.4 jit_solution(6415348061224779753)
XLA Ops:
  0.6 146.6 %window.1 = (f32[64,32,512]{2,1,0:T(8,128)}, f32[512,512]{1,0:T(8,128)}, f32[512,512]{1,0:T(8,128)}) custom-call(s32[1,128]{1,0:T(1,128)} %bitcast.1, bf16[128,128,128]{2,1,0:T(8,128)(2,1)} %x_hbm.1, bf16[128,128,128]{2,1,0:T(8,128)(2,1)} %y_hbm.1), custom_call_target="tpu_custom_call" | custom-call | tf_op jit(solution)/shard_map/window/pallas_call | solution.py:433
  147.2 0.0 copy-start.1
  147.3 0.0 copy-start
  147.3 5.2 %copy.9 = f32[64,32,512]{2,1,0:T(8,128)} copy(f32[64,32,512]{2,1,0:T(8,128)} %get-tuple-element.6) | data formatting | bytes 8388608
  152.4 0.0 copy-done.1
  152.4 1.0 copy.10
  153.4 0.0 copy-done
  153.4 1.0 copy.11
Async XLA Ops:
  147.2 5.2 %copy-start.1 = (f32[512,512]{1,0:T(8,128)S(1)}, f32[512,512]{1,0:T(8,128)}, u32[]{:S(2)}) copy-start(f32[512,512]{1,0:T(8,128)} %get-tuple-element.7) | copy-start | bytes 3145732
  147.3 6.1 %copy-start = (f32[512,512]{1,0:T(8,128)S(1)}, f32[512,512]{1,0:T(8,128)}, u32[]{:S(2)}) copy-start(f32[512,512]{1,0:T(8,128)} %get-tuple-element.8) | copy-start | bytes 3145732

commit v3 on v2

--- a/solution.py
+++ b/solution.py
@@ -109,8 +109,11 @@
 BF16 = jnp.bfloat16
 ORDER = (0, 2, 1, 3)
 CHUNKS = 8
-GT = 160
+EARLY = 5
+FIRST_Y = 2
 CT = 256
+G_GROUPS = ((0, 64), (64, 96))
+C_GROUPS = ((0, 64), (64, 64), (128, 64), (192, 64))
 
 
 def where_am_i():
@@ -164,63 +167,87 @@
     return slot, block
 
 
-def all_sum(n, tiles, b1, half, b2, piece, zb, half2, full, s1, r1, s2, r2, s3, r3, s4, r4, s5, r5, after_z=None):
+def all_sum(groups, tiles, b1, half, b2, piece, zb, half2, full, s1, r1, s2, r2, s3, r3, s4, r4, s5, r5, after_scatter=None, after_z=None):
     y, x, c, z, s = where_am_i()
     chip = s // 2
-    h, m = n // 2, n // 32
     mate = chip * 2 + (1 - c)
-    cp1 = remote(tiles.at[pl.ds((1 - c) * h, h)], b1, s1.at[0], r1.at[0], space=mate)
-    cp1.start()
-    cp1.wait_recv()
-    half[...] = tiles[pl.ds(c * h, h)] + b1[...]
 
     def chip_at(d):
         return lax.rem(y + d // 4, 4) * 4 + lax.rem(x + lax.rem(d, 4), 4)
 
-    def scatter(d):
+    spans = [(g, at, n // 2, n // 32) for g, (at, n) in enumerate(groups)]
+
+    def swap(g, at, h, m):
+        return remote(tiles.at[pl.ds(at + (1 - c) * h, h)], b1.at[at // 2:at // 2 + h], s1.at[g], r1.at[g], space=mate)
+
+    def scatter(g, at, h, m, d):
         q = chip_at(d)
-        return remote(half.at[pl.ds(q * m, m)], b2.at[chip], s2.at[d], r2.at[d], space=q * 2 + c)
-
-    loop(1, 16, lambda d: scatter(d).start())
-    b2[chip] = half[pl.ds(chip * m, m)]
-    loop(1, 16, lambda d: scatter(d).wait_recv())
-    total = b2[0]
-    for q in range(1, 16):
-        total = total + b2[q]
-    piece[...] = total
-    zcp = [remote(piece, zb.at[z], s3.at[d - 1], r3.at[d - 1], snap=lax.rem(z + d, 4)) for d in (1, 2, 3)]
-    for cp in zcp:
-        cp.start()
+        return remote(half.at[pl.ds(at // 2 + q * m, m)], b2.at[chip, at // 32:at // 32 + m], s2.at[g, d], r2.at[g, d], space=q * 2 + c)
+
+    def across(g, at, h, m, d):
+        mine = pl.ds(at // 32, m)
+        return remote(piece.at[mine], zb.at[z, mine], s3.at[g, d], r3.at[g, d], snap=lax.rem(z + d, 4))
+
+    def gather(g, at, h, m, d):
+        mine = pl.ds(at // 2 + chip * m, m)
+        return remote(half2.at[mine], half2.at[mine], s4.at[g, d], r4.at[g, d], space=chip_at(d) * 2 + c)
+
+    def swap_back(g, at, h, m):
+        return remote(half2.at[at // 2:at // 2 + h], full.at[pl.ds(at + c * h, h)], s5.at[g], r5.at[g], space=mate)
+
+    for sp in spans:
+        swap(*sp).start()
+    for sp in spans:
+        g, at, h, m = sp
+        swap(*sp).wait_recv()
+        half[at // 2:at // 2 + h] = tiles[pl.ds(at + c * h, h)] + b1[at // 2:at // 2 + h]
+        loop(1, 16, lambda d: scatter(*sp, d).start())
+        b2[chip, at // 32:at // 32 + m] = half[pl.ds(at // 2 + chip * m, m)]
+    if after_scatter is not None:
+        after_scatter()
+    for sp in spans:
+        g, at, h, m = sp
+        loop(1, 16, lambda d: scatter(*sp, d).wait_recv())
+        mine = slice(at // 32, at // 32 + m)
+        total = b2[0, mine]
+        for q in range(1, 16):
+            total = total + b2[q, mine]
+        piece[mine] = total
+        for d in (1, 2, 3):
+            across(*sp, d).start()
+        zb[z, mine] = piece[mine]
     if after_z is not None:
         after_z()
-    zb[z] = piece[...]
-    for cp in zcp:
-        cp.wait_recv()
-    half2[pl.ds(chip * m, m)] = zb[0] + zb[1] + zb[2] + zb[3]
-
-    def gather(d):
-        mine = pl.ds(chip * m, m)
-        return remote(half2.at[mine], half2.at[mine], s4.at[d], r4.at[d], space=chip_at(d) * 2 + c)
-
-    loop(1, 16, lambda d: gather(d).start())
-    loop(1, 16, lambda d: gather(d).wait_recv())
-    cp5 = remote(half2, full.at[pl.ds(c * h, h)], s5.at[0], r5.at[0], space=mate)
-    cp5.start()
-    full[pl.ds(c * h, h)] = half2[...]
-    cp5.wait_recv()
+    for sp in spans:
+        g, at, h, m = sp
+        for d in (1, 2, 3):
+            across(*sp, d).wait_recv()
+        mine = slice(at // 32, at // 32 + m)
+        half2[pl.ds(at // 2 + chip * m, m)] = zb[0, mine] + zb[1, mine] + zb[2, mine] + zb[3, mine]
+        loop(1, 16, lambda d: gather(*sp, d).start())
+    for sp in spans:
+        g, at, h, m = sp
+        loop(1, 16, lambda d: gather(*sp, d).wait_recv())
+        swap_back(*sp).start()
+        full[pl.ds(at + c * h, h)] = half2[at // 2:at // 2 + h]
+    for sp in spans:
+        swap_back(*sp).wait_recv()
 
     def drain():
-        cp1.wait_send()
-        loop(1, 16, lambda d: scatter(d).wait_send())
-        for cp in zcp:
-            cp.wait_send()
-        loop(1, 16, lambda d: gather(d).wait_send())
-        cp5.wait_send()
+        for sp in spans:
+            swap(*sp).wait_send()
+            loop(1, 16, lambda d: scatter(*sp, d).wait_send())
+            for d in (1, 2, 3):
+                across(*sp, d).wait_send()
+            loop(1, 16, lambda d: gather(*sp, d).wait_send())
+            swap_back(*sp).wait_send()
 
     return drain
 
 
-def sum_scratch(n):
+def sum_scratch(groups):
+    n = sum(size for _, size in groups)
+    k = len(groups)
     h, m = n // 2, n // 32
     dma = pltpu.SemaphoreType.DMA
     return [
@@ -232,12 +259,12 @@
         pltpu.VMEM((4, m, 8, 128), F32),
         pltpu.VMEM((h, 8, 128), F32),
         pltpu.VMEM((n, 8, 128), F32),
-        dma((1,)), dma((1,)), dma((16,)), dma((16,)), dma((3,)), dma((3,)), dma((16,)), dma((16,)), dma((1,)), dma((1,)),
+        dma((k,)), dma((k,)), dma((k, 16)), dma((k, 16)), dma((k, 4)), dma((k, 4)), dma((k, 16)), dma((k, 16)), dma((k,)), dma((k,)),
     ]
 
 
-def whole(dest, x_hbm, y_hbm, q_hbm, r_out, p_out, xin, yin, xo, yo, xr, yr, sr, xs, qv, acc, M, W, wk, rk,
-          ids, tab_v, tab_s, at_v, at_s, lsem, tsem, qsem, xs_s, xs_r, ys_s, ys_r, sp_s, sp_r, id_s, id_r, *sums):
+def whole(dest, x_hbm, y_hbm, q_hbm, r_out, w_out, c_out, xin, yin, xo, yo, xr, yr, sr, xs, qv, acc, M, W, R, wp, wk, rk,
+          ids, tab_v, tab_s, at_v, at_s, lsem, tsem, qsem, osem, xs_s, xs_r, ys_s, ys_r, sp_s, sp_r, id_s, id_r, *sums):
     y, x, c, z, s = where_am_i()
     gsum, csum = sums[:18], sums[18:]
     load_x = pltpu.make_async_copy(x_hbm, xin.at[pl.ds(0, 128)], lsem.at[0])
@@ -302,7 +329,8 @@
     for o in range(1, 32):
         send_ids(o // 4, o % 4).start()
     loop(1, CHUNKS, lambda k: order_slots(yin, yo, yr, k))
-    send_z(yo, yr, ys_s, ys_r, 0)
+    for k in range(FIRST_Y):
+        send_z(yo, yr, ys_s, ys_r, k)
 
     for o in range(1, 32):
         send_ids(o // 4, o % 4).wait_recv()
@@ -329,27 +357,31 @@
     acc[...] = jnp.zeros((512, 512), F32)
     contract = (((0,), (0,)), ((), ()))
 
+    def forward(k):
+        for j in range(4):
+            to_slab(k, j).start()
+
     def gram_step(k):
         for cp in over_z(xo, xr, xs_s, xs_r, k):
             cp.wait_recv()
-        for j in range(4):
-            if j == 0:
-                @pl.when(k > 0)
-                def _():
-                    to_slab(k, 0).start()
-
-                @pl.when(k == 0)
-                def _():
-                    sr[:, pl.ds(4 * s, 4)] = xr[:, 0:4]
-            else:
-                to_slab(k, j).start()
+
+        @pl.when(k == 0)
+        def _():
+            sr[:, pl.ds(4 * s, 4)] = xr[:, 0:4]
+            for j in range(1, 4):
+                to_slab(0, j).start()
+
+        @pl.when((k > 0) & (k < EARLY))
+        def _():
+            forward(k)
+
         rows = panel_rows(xr, k)
         acc[...] += lax.dot_general(rows, rows, contract, preferred_element_type=F32)
 
     loop(0, CHUNKS, gram_step)
 
     def later_y():
-        for k in range(1, CHUNKS):
+        for k in range(FIRST_Y, CHUNKS):
             send_z(yo, yr, ys_s, ys_r, k)
 
     b = 0
@@ -357,43 +389,49 @@
         for j in range(i, 4):
             gsum[0][16 * b:16 * b + 16] = acc[128 * i:128 * i + 128, 128 * j:128 * j + 128].reshape(16, 8, 128)
             b += 1
-    drain_g = all_sum(GT, *gsum, after_z=later_y)
+    drain_g = all_sum(G_GROUPS, *gsum, after_z=later_y)
+    loop(EARLY, CHUNKS, forward)
     full = gsum[7]
     b = 0
     for i in range(4):
         for j in range(i, 4):
             M[128 * i:128 * i + 128, 128 * j:128 * j + 128] = full[16 * b:16 * b + 16].reshape(128, 128) * (1.0 / ROWS)
             b += 1
-    factor(M, r_out, W, wk, rk)
-
-    for o in range(1, 32):
-        to_slab(o // 4, o % 4).wait_recv()
-
-    def pick_block(i):
-        at = at_s[0, i]
-        for p in range(4):
-            xs[i, :, 128 * p:128 * p + 128] = sr[p, at]
-
-    loop(0, BLK_DEV, pick_block)
-    w1 = W[...].astype(BF16)
-    w2 = (W[...] - w1.astype(F32)).astype(BF16)
-    w3 = (W[...] - w1.astype(F32) - w2.astype(F32)).astype(BF16)
+    factor(M, R, W, wk, rk)
+    out_r = pltpu.make_async_copy(R, r_out, osem.at[0])
+    out_w = pltpu.make_async_copy(wp, w_out, osem.at[1])
+    out_r.start()
+    wp[0] = W[...].astype(BF16)
+    wp[1] = (W[...] - wp[0].astype(F32)).astype(BF16)
+    wp[2] = (W[...] - wp[0].astype(F32) - wp[1].astype(F32)).astype(BF16)
+    out_w.start()
+
     last = (((1,), (1,)), ((), ()))
 
     def store_q(i):
         span = pl.ds(16 * i, 16)
         return pltpu.make_async_copy(qv.at[span], q_hbm.at[span], qsem.at[i])
 
-    def basis(i):
-        span = pl.ds(16 * i, 16)
-        rows = xs[span].reshape(512, 512)
-        out = lax.dot_general(rows, w3, last, preferred_element_type=F32)
-        out = out + lax.dot_general(rows, w2, last, preferred_element_type=F32)
-        out = out + lax.dot_general(rows, w1, last, preferred_element_type=F32)
-        qv[span] = out.reshape(16, 32, 512)
-        store_q(i).start()
-
-    loop(0, 4, basis)
+    def form_basis():
+        for o in range(1, 32):
+            to_slab(o // 4, o % 4).wait_recv()
+
+        def pick_block(i):
+            at = at_s[0, i]
+            for p in range(4):
+                xs[i, :, 128 * p:128 * p + 128] = sr[p, at]
+
+        loop(0, BLK_DEV, pick_block)
+        def basis(i):
+            span = pl.ds(16 * i, 16)
+            rows = xs[span].reshape(512, 512)
+            out = lax.dot_general(rows, wp[2], last, preferred_element_type=F32)
+            out = out + lax.dot_general(rows, wp[1], last, preferred_element_type=F32)
+            out = out + lax.dot_general(rows, wp[0], last, preferred_element_type=F32)
+            qv[span] = out.reshape(16, 32, 512)
+            store_q(i).start()
+
+        loop(0, 4, basis)
 
     acc[...] = jnp.zeros((512, 512), F32)
 
@@ -405,12 +443,9 @@
     loop(0, CHUNKS, cross_step)
     for j in range(4):
         csum[0][64 * j:64 * j + 64] = acc[:, 128 * j:128 * j + 128].reshape(64, 8, 128)
-    drain_c = all_sum(CT, *csum)
-    for j in range(4):
-        M[:, 128 * j:128 * j + 128] = csum[7][64 * j:64 * j + 64].reshape(512, 128)
-    p_out[...] = jnp.dot(W[...], M[...], precision=HI, preferred_element_type=F32) * (1.0 / 512.0)
-
-    loop(0, 4, lambda i: store_q(i).wait())
+    drain_c = all_sum(C_GROUPS, *csum, after_scatter=form_basis)
+    out_c = pltpu.make_async_copy(csum[7], c_out, osem.at[2])
+    out_c.start()
     drain_g()
     drain_c()
     for o in range(1, 32):
@@ -422,6 +457,54 @@
             cp.wait_send()
 
     loop(0, CHUNKS, drain_z)
+    loop(0, 4, lambda i: store_q(i).wait())
+    out_r.wait()
+    out_w.wait()
+    out_c.wait()
+
+
+def finish(q_in, r_in, w_in, c_in, q_out, r_out, p_out, qv, R, W, C, cp, p, qi, qo, ii, oo):
+    get_c = pltpu.make_async_copy(c_in, C, ii.at[0])
+    get_w = pltpu.make_async_copy(w_in, W, ii.at[1])
+    get_r = pltpu.make_async_copy(r_in, R, ii.at[2])
+    parts = [pl.ds(16 * i, 16) for i in range(4)]
+    gets = [pltpu.make_async_copy(q_in.at[t], qv.at[t], qi.at[i]) for i, t in enumerate(parts)]
+    puts = [pltpu.make_async_copy(qv.at[t], q_out.at[t], qo.at[i]) for i, t in enumerate(parts)]
+    put_r = pltpu.make_async_copy(R, r_out, oo.at[0])
+    put_p = pltpu.make_async_copy(p, p_out, oo.at[1])
+    get_c.start()
+    get_w.start()
+    for copy in gets:
+        copy.start()
+    get_r.start()
+    get_c.wait()
+    for j in range(4):
+        rows = C[64 * j:64 * j + 64].reshape(512, 128)
+        span = slice(128 * j, 128 * j + 128)
+        c1 = rows.astype(BF16)
+        c2 = (rows - c1.astype(F32)).astype(BF16)
+        cp[0, :, span] = c1
+        cp[1, :, span] = c2
+        cp[2, :, span] = (rows - c1.astype(F32) - c2.astype(F32)).astype(BF16)
+    get_w.wait()
+
+    def term(i, j):
+        return jnp.dot(W[i], cp[j], preferred_element_type=F32)
+
+    for i in range(2):
+        gets[i].wait()
+        puts[i].start()
+    p[...] = (term(2, 0) + term(0, 2) + term(1, 1) + term(1, 0) + term(0, 1) + term(0, 0)) * (1.0 / 512.0)
+    put_p.start()
+    for i in range(2, 4):
+        gets[i].wait()
+        puts[i].start()
+    get_r.wait()
+    put_r.start()
+    for copy in puts:
+        copy.wait()
+    put_r.wait()
+    put_p.wait()
 
 
 def body(owned_x, owned_y, patch_dest):
@@ -430,11 +513,11 @@
     dma = pltpu.SemaphoreType.DMA
     square = jax.ShapeDtypeStruct((512, 512), F32)
     panels = pltpu.VMEM((4, 128, 32, 128), BF16)
-    return pl.pallas_call(
+    basis, upper, inverse, cross = pl.pallas_call(
         whole,
-        out_shape=(jax.ShapeDtypeStruct((BLK_DEV, 32, 512), F32), square, square),
+        out_shape=(jax.ShapeDtypeStruct((BLK_DEV, 32, 512), F32), square, jax.ShapeDtypeStruct((3, 512, 512), BF16), jax.ShapeDtypeStruct((CT, 8, 128), F32)),
         in_specs=[V, A, A],
-        out_specs=(A, V, V),
+        out_specs=(A, A, A, A),
         scratch_shapes=[
             pltpu.VMEM((129, 128, 128), BF16),
             pltpu.VMEM((129, 128, 128), BF16),
@@ -444,6 +527,8 @@
             pltpu.VMEM((512, 512), F32),
             pltpu.VMEM((512, 512), F32),
             pltpu.VMEM((512, 512), F32),
+            pltpu.VMEM((512, 512), F32),
+            pltpu.VMEM((3, 512, 512), BF16),
             pltpu.VMEM((128, 128), F32),
             pltpu.VMEM((128, 128), F32),
             pltpu.VMEM((32, 8, 128), jnp.int32),
@@ -451,15 +536,32 @@
             pltpu.SMEM((8, 128), jnp.int32),
             pltpu.VMEM((8, 128), jnp.int32),
             pltpu.SMEM((8, 128), jnp.int32),
-            dma((2,)), dma((2,)), dma((4,)),
+            dma((2,)), dma((2,)), dma((4,)), dma((3,)),
             dma((CHUNKS, 3)), dma((CHUNKS, 3)), dma((CHUNKS, 3)), dma((CHUNKS, 3)),
             dma((32,)), dma((32,)), dma((32,)), dma((32,)),
-        ] + sum_scratch(GT) + sum_scratch(CT),
+        ] + sum_scratch(G_GROUPS) + sum_scratch(C_GROUPS),
         compiler_params=pltpu.CompilerParams(
             collective_id=0, has_side_effects=True, vmem_limit_bytes=63 << 20
         ),
         name="window",
     )(patch_dest.reshape(1, 128), owned_x, owned_y)
+    return pl.pallas_call(
+        finish,
+        out_shape=(jax.ShapeDtypeStruct((BLK_DEV, 32, 512), F32), square, square),
+        in_specs=[A, A, A, A],
+        out_specs=(A, A, A),
+        scratch_shapes=[
+            pltpu.VMEM((BLK_DEV, 32, 512), F32),
+            pltpu.VMEM((512, 512), F32),
+            pltpu.VMEM((3, 512, 512), BF16),
+            pltpu.VMEM((CT, 8, 128), F32),
+            pltpu.VMEM((3, 512, 512), BF16),
+            pltpu.VMEM((512, 512), F32),
+            dma((4,)), dma((4,)), dma((3,)), dma((2,)),
+        ],
+        compiler_params=pltpu.CompilerParams(vmem_limit_bytes=63 << 20),
+        name="finish",
+    )(basis, upper, inverse, cross)
 
 
 def solution(mesh):

time: 154 us -> 141 us (0.916)
  local copies, waits for them, and re-layouts: 7.1 us -> 0 us
  Pallas kernels: 147 us -> 140 us
    pallas_call x1, Pallas kernels: 147 us -> 134 us  [body(): pl.pallas_call(whole, out_shape=(jax.ShapeDtypeStruct((BLK_DEV, 32, 512),...]
    unnamed x7 -> x0, local copies, waits for them, and re-layouts: 7.1 us -> none
    pallas_call x0 -> x1, Pallas kernels: none -> 6.27 us  [body(): pl.pallas_call(finish, out_shape=(jax.ShapeDtypeStruct((BLK_DEV, 32, 512)...]
where the time goes in v3:
time: 141 us
  Pallas kernels  140 us (99%)
    pallas_call x1, Pallas kernels, body(): pl.pallas_call(whole, out_shape=(jax.ShapeDtypeStruct((BLK_DEV, 32, 512),...  134 us
    pallas_call x1, Pallas kernels, body(): pl.pallas_call(finish, out_shape=(jax.ShapeDtypeStruct((BLK_DEV, 32, 512)...  6.27 us

profile of v3, /device:TPU:1, one launch (start us, length us, event | category | flops | bytes accessed | tf_op | source)
XLA Modules:
  0.0 140.9 jit_solution(9948625926264982270)
XLA Ops:
  0.6 134.0 %window.1 = (f32[64,32,512]{2,1,0:T(8,128)}, f32[512,512]{1,0:T(8,128)}, bf16[3,512,512]{2,1,0:T(8,128)(2,1)}, f32[256,8,128]{2,1,0:T(8,128)}) custom-call(s32[1,128]{1,0:T(1,128)} %bitcast.1, bf16[128,128,128]{2,1,0:T(8,128)(2,1)} %x_hbm.1, bf16[128,128,128]{2,1,0:T(8,128)(2,1)} %y_hbm.1), custom_call_target="tpu_custom_call" | custom-call | tf_op jit(solution)/shard_map/window/pallas_call | solution.py:516
  134.6 6.3 %finish.1 = (f32[64,32,512]{2,1,0:T(8,128)}, f32[512,512]{1,0:T(8,128)}, f32[512,512]{1,0:T(8,128)}) custom-call(f32[64,32,512]{2,1,0:T(8,128)} %get-tuple-element.7.q_in, f32[512,512]{1,0:T(8,128)} %get-tuple-element.8.r_in, bf16[3,512,512]{2,1,0:T(8,128)(2,1)} %get-tuple-element.9.w_in, f32[256,8,128]{2,1,0:T(8,128)} %get-tuple-element.10.c_in), custom_call_target="tpu_custom_call" | custom-call | tf_op jit(solution)/shard_map/finish/pallas_call | solution.py:548

commit v4 on v3

--- a/solution.py
+++ b/solution.py
@@ -144,6 +144,10 @@
     lax.fori_loop(lo, hi, step, 0)
 
 
+def await_bytes(ref, sem):
+    pltpu.make_async_copy(ref, ref, sem).wait()
+
+
 def column(row):
     eye = lax.broadcasted_iota(jnp.int32, (128, 128), 0) == lax.broadcasted_iota(jnp.int32, (128, 128), 1)
     return jnp.sum(jnp.where(eye, jnp.broadcast_to(row, (128, 128)), 0), axis=1, keepdims=True)
@@ -167,7 +171,7 @@
     return slot, block
 
 
-def all_sum(groups, tiles, b1, half, b2, piece, zb, half2, full, s1, r1, s2, r2, s3, r3, s4, r4, s5, r5, after_scatter=None, after_z=None):
+def all_sum(groups, tiles, b1, half, b2, piece, zb, half2, full, ss, r1, r2, r3, r4, r5, after_scatter=None, after_z=None):
     y, x, c, z, s = where_am_i()
     chip = s // 2
     mate = chip * 2 + (1 - c)
@@ -178,22 +182,22 @@
     spans = [(g, at, n // 2, n // 32) for g, (at, n) in enumerate(groups)]
 
     def swap(g, at, h, m):
-        return remote(tiles.at[pl.ds(at + (1 - c) * h, h)], b1.at[at // 2:at // 2 + h], s1.at[g], r1.at[g], space=mate)
+        return remote(tiles.at[pl.ds(at + (1 - c) * h, h)], b1.at[at // 2:at // 2 + h], ss.at[0], r1.at[g], space=mate)
 
     def scatter(g, at, h, m, d):
         q = chip_at(d)
-        return remote(half.at[pl.ds(at // 2 + q * m, m)], b2.at[chip, at // 32:at // 32 + m], s2.at[g, d], r2.at[g, d], space=q * 2 + c)
+        return remote(half.at[pl.ds(at // 2 + q * m, m)], b2.at[chip, at // 32:at // 32 + m], ss.at[1], r2.at[g], space=q * 2 + c)
 
     def across(g, at, h, m, d):
         mine = pl.ds(at // 32, m)
-        return remote(piece.at[mine], zb.at[z, mine], s3.at[g, d], r3.at[g, d], snap=lax.rem(z + d, 4))
+        return remote(piece.at[mine], zb.at[z, mine], ss.at[2], r3.at[g], snap=lax.rem(z + d, 4))
 
     def gather(g, at, h, m, d):
         mine = pl.ds(at // 2 + chip * m, m)
-        return remote(half2.at[mine], half2.at[mine], s4.at[g, d], r4.at[g, d], space=chip_at(d) * 2 + c)
+        return remote(half2.at[mine], half2.at[mine], ss.at[3], r4.at[g], space=chip_at(d) * 2 + c)
 
     def swap_back(g, at, h, m):
-        return remote(half2.at[at // 2:at // 2 + h], full.at[pl.ds(at + c * h, h)], s5.at[g], r5.at[g], space=mate)
+        return remote(half2.at[at // 2:at // 2 + h], full.at[pl.ds(at + c * h, h)], ss.at[4], r5.at[g], space=mate)
 
     for sp in spans:
         swap(*sp).start()
@@ -207,8 +211,8 @@
         after_scatter()
     for sp in spans:
         g, at, h, m = sp
-        loop(1, 16, lambda d: scatter(*sp, d).wait_recv())
         mine = slice(at // 32, at // 32 + m)
+        await_bytes(b2.at[0:15, mine], r2.at[g])
         total = b2[0, mine]
         for q in range(1, 16):
             total = total + b2[q, mine]
@@ -220,27 +224,21 @@
         after_z()
     for sp in spans:
         g, at, h, m = sp
-        for d in (1, 2, 3):
-            across(*sp, d).wait_recv()
         mine = slice(at // 32, at // 32 + m)
+        await_bytes(zb.at[0:3, mine], r3.at[g])
         half2[pl.ds(at // 2 + chip * m, m)] = zb[0, mine] + zb[1, mine] + zb[2, mine] + zb[3, mine]
         loop(1, 16, lambda d: gather(*sp, d).start())
     for sp in spans:
         g, at, h, m = sp
-        loop(1, 16, lambda d: gather(*sp, d).wait_recv())
+        await_bytes(b2.at[0:15, at // 32:at // 32 + m], r4.at[g])
         swap_back(*sp).start()
         full[pl.ds(at + c * h, h)] = half2[at // 2:at // 2 + h]
     for sp in spans:
         swap_back(*sp).wait_recv()
 
     def drain():
-        for sp in spans:
-            swap(*sp).wait_send()
-            loop(1, 16, lambda d: scatter(*sp, d).wait_send())
-            for d in (1, 2, 3):
-                across(*sp, d).wait_send()
-            loop(1, 16, lambda d: gather(*sp, d).wait_send())
-            swap_back(*sp).wait_send()
+        for stage, sent in enumerate((b1, b2.at[0:15], zb.at[0:3], b2.at[0:15], b1)):
+            await_bytes(sent, ss.at[stage])
 
     return drain
 
@@ -259,14 +257,14 @@
         pltpu.VMEM((4, m, 8, 128), F32),
         pltpu.VMEM((h, 8, 128), F32),
         pltpu.VMEM((n, 8, 128), F32),
-        dma((k,)), dma((k,)), dma((k, 16)), dma((k, 16)), dma((k, 4)), dma((k, 4)), dma((k, 16)), dma((k, 16)), dma((k,)), dma((k,)),
+        dma((5,)), dma((k,)), dma((k,)), dma((k,)), dma((k,)), dma((k,)),
     ]
 
 
 def whole(dest, x_hbm, y_hbm, q_hbm, r_out, w_out, c_out, xin, yin, xo, yo, xr, yr, sr, xs, qv, acc, M, W, R, wp, wk, rk,
           ids, tab_v, tab_s, at_v, at_s, lsem, tsem, qsem, osem, xs_s, xs_r, ys_s, ys_r, sp_s, sp_r, id_s, id_r, *sums):
     y, x, c, z, s = where_am_i()
-    gsum, csum = sums[:18], sums[18:]
+    gsum, csum = sums[:14], sums[14:]
     load_x = pltpu.make_async_copy(x_hbm, xin.at[pl.ds(0, 128)], lsem.at[0])
     load_y = pltpu.make_async_copy(y_hbm, yin.at[pl.ds(0, 128)], lsem.at[1])
     load_x.start()
@@ -306,7 +304,7 @@
         out = []
         for d in (1, 2, 3):
             to = lax.rem(z + d, 4)
-            out.append(remote(src.at[to, span], recv.at[z, span], ss.at[k, d - 1], rs.at[k, d - 1], snap=to))
+            out.append(remote(src.at[to, span], recv.at[z, span], ss.at[0], rs.at[k], snap=to))
         return out
 
     def send_z(src, recv, ss, rs, k):
@@ -323,8 +321,7 @@
     send_z(xo, xr, xs_s, xs_r, CHUNKS - 1)
 
     def send_ids(k, j):
-        o = 4 * k + j
-        return remote(ids.at[s], ids.at[s], id_s.at[o], id_r.at[o], space=space_at(k, j))
+        return remote(ids.at[s], ids.at[s], id_s.at[0], id_r.at[0], space=space_at(k, j))
 
     for o in range(1, 32):
         send_ids(o // 4, o % 4).start()
@@ -332,8 +329,7 @@
     for k in range(FIRST_Y):
         send_z(yo, yr, ys_s, ys_r, k)
 
-    for o in range(1, 32):
-        send_ids(o // 4, o % 4).wait_recv()
+    await_bytes(ids.at[0:31], id_r.at[0])
     wanted = s * BLK_DEV + lax.broadcasted_iota(jnp.int32, (BLK_DEV, 1), 0)
     place = lax.rem(lax.broadcasted_iota(jnp.int32, (1, 128), 1), 4)
     found = jnp.zeros((BLK_DEV, 128), jnp.int32)
@@ -349,7 +345,7 @@
 
     def to_slab(k, j):
         o = 4 * k + j
-        return remote(xr.at[:, pl.ds(4 * o, 4)], sr.at[:, pl.ds(4 * s, 4)], sp_s.at[o], sp_r.at[o], space=space_at(k, j))
+        return remote(xr.at[:, pl.ds(4 * o, 4)], sr.at[:, pl.ds(4 * s, 4)], sp_s.at[0], sp_r.at[0], space=space_at(k, j))
 
     def panel_rows(buf, k):
         return jnp.concatenate([buf[p, pl.ds(16 * k, 16)].reshape(512, 128) for p in range(4)], axis=1)
@@ -362,8 +358,7 @@
             to_slab(k, j).start()
 
     def gram_step(k):
-        for cp in over_z(xo, xr, xs_s, xs_r, k):
-            cp.wait_recv()
+        await_bytes(xr.at[0:3, pl.ds(16 * k, 16)], xs_r.at[k])
 
         @pl.when(k == 0)
         def _():
@@ -413,8 +408,7 @@
         return pltpu.make_async_copy(qv.at[span], q_hbm.at[span], qsem.at[i])
 
     def form_basis():
-        for o in range(1, 32):
-            to_slab(o // 4, o % 4).wait_recv()
+        await_bytes(sr.at[:, 0:124], sp_r.at[0])
 
         def pick_block(i):
             at = at_s[0, i]
@@ -436,8 +430,7 @@
     acc[...] = jnp.zeros((512, 512), F32)
 
     def cross_step(k):
-        for cp in over_z(yo, yr, ys_s, ys_r, k):
-            cp.wait_recv()
+        await_bytes(yr.at[0:3, pl.ds(16 * k, 16)], ys_r.at[k])
         acc[...] += lax.dot_general(panel_rows(xr, k), panel_rows(yr, k), contract, preferred_element_type=F32)
 
     loop(0, CHUNKS, cross_step)
@@ -448,15 +441,10 @@
     out_c.start()
     drain_g()
     drain_c()
-    for o in range(1, 32):
-        send_ids(o // 4, o % 4).wait_send()
-        to_slab(o // 4, o % 4).wait_send()
-
-    def drain_z(k):
-        for cp in over_z(xo, xr, xs_s, xs_r, k) + over_z(yo, yr, ys_s, ys_r, k):
-            cp.wait_send()
-
-    loop(0, CHUNKS, drain_z)
+    await_bytes(ids.at[0:31], id_s.at[0])
+    await_bytes(sr.at[:, 0:124], sp_s.at[0])
+    await_bytes(xo.at[0:3], xs_s.at[0])
+    await_bytes(yo.at[0:3], ys_s.at[0])
     loop(0, 4, lambda i: store_q(i).wait())
     out_r.wait()
     out_w.wait()
@@ -537,8 +525,8 @@
             pltpu.VMEM((8, 128), jnp.int32),
             pltpu.SMEM((8, 128), jnp.int32),
             dma((2,)), dma((2,)), dma((4,)), dma((3,)),
-            dma((CHUNKS, 3)), dma((CHUNKS, 3)), dma((CHUNKS, 3)), dma((CHUNKS, 3)),
-            dma((32,)), dma((32,)), dma((32,)), dma((32,)),
+            dma((1,)), dma((CHUNKS,)), dma((1,)), dma((CHUNKS,)),
+            dma((1,)), dma((1,)), dma((1,)), dma((1,)),
         ] + sum_scratch(G_GROUPS) + sum_scratch(C_GROUPS),
         compiler_params=pltpu.CompilerParams(
             collective_id=0, has_side_effects=True, vmem_limit_bytes=63 << 20

time: 141 us -> 135 us (0.957)
  Pallas kernels: 140 us -> 134 us
    pallas_call x1, Pallas kernels: 134 us -> 128 us  [body(): pl.pallas_call(whole, out_shape=(jax.ShapeDtypeStruct((BLK_DEV, 32, 512),...]
where the time goes in v4:
time: 135 us
  Pallas kernels  134 us (99%)
    pallas_call x1, Pallas kernels, body(): pl.pallas_call(whole, out_shape=(jax.ShapeDtypeStruct((BLK_DEV, 32, 512),...  128 us
    pallas_call x1, Pallas kernels, body(): pl.pallas_call(finish, out_shape=(jax.ShapeDtypeStruct((BLK_DEV, 32, 512)...  6.27 us

profile of v4, /device:TPU:1, one launch (start us, length us, event | category | flops | bytes accessed | tf_op | source)
XLA Modules:
  0.0 134.7 jit_solution(9383506476554663332)
XLA Ops:
  0.6 127.8 %window.1 = (f32[64,32,512]{2,1,0:T(8,128)}, f32[512,512]{1,0:T(8,128)}, bf16[3,512,512]{2,1,0:T(8,128)(2,1)}, f32[256,8,128]{2,1,0:T(8,128)}) custom-call(s32[1,128]{1,0:T(1,128)} %bitcast.1, bf16[128,128,128]{2,1,0:T(8,128)(2,1)} %x_hbm.1, bf16[128,128,128]{2,1,0:T(8,128)(2,1)} %y_hbm.1), custom_call_target="tpu_custom_call" | custom-call | tf_op jit(solution)/shard_map/window/pallas_call | solution.py:504
  128.5 6.3 %finish.1 = (f32[64,32,512]{2,1,0:T(8,128)}, f32[512,512]{1,0:T(8,128)}, f32[512,512]{1,0:T(8,128)}) custom-call(f32[64,32,512]{2,1,0:T(8,128)} %get-tuple-element.7.q_in, f32[512,512]{1,0:T(8,128)} %get-tuple-element.8.r_in, bf16[3,512,512]{2,1,0:T(8,128)(2,1)} %get-tuple-element.9.w_in, f32[256,8,128]{2,1,0:T(8,128)} %get-tuple-element.10.c_in), custom_call_target="tpu_custom_call" | custom-call | tf_op jit(solution)/shard_map/finish/pallas_call | solution.py:536

commit v5 on v4

--- a/solution.py
+++ b/solution.py
@@ -171,7 +171,7 @@
     return slot, block
 
 
-def all_sum(groups, tiles, b1, half, b2, piece, zb, half2, full, ss, r1, r2, r3, r4, r5, after_scatter=None, after_z=None):
+def all_sum(groups, tiles, b1, half, b2, piece, zb, half2, full, ss, r1, r2, r3, r4, r5, keep, after_scatter=None, after_z=None):
     y, x, c, z, s = where_am_i()
     chip = s // 2
     mate = chip * 2 + (1 - c)
@@ -232,7 +232,7 @@
         g, at, h, m = sp
         await_bytes(b2.at[0:15, at // 32:at // 32 + m], r4.at[g])
         swap_back(*sp).start()
-        full[pl.ds(at + c * h, h)] = half2[at // 2:at // 2 + h]
+        keep(half2.at[at // 2:at // 2 + h], full.at[pl.ds(at + c * h, h)])
     for sp in spans:
         swap_back(*sp).wait_recv()
 
@@ -243,7 +243,7 @@
     return drain
 
 
-def sum_scratch(groups):
+def sum_scratch(groups, with_full):
     n = sum(size for _, size in groups)
     k = len(groups)
     h, m = n // 2, n // 32
@@ -256,9 +256,7 @@
         pltpu.VMEM((m, 8, 128), F32),
         pltpu.VMEM((4, m, 8, 128), F32),
         pltpu.VMEM((h, 8, 128), F32),
-        pltpu.VMEM((n, 8, 128), F32),
-        dma((5,)), dma((k,)), dma((k,)), dma((k,)), dma((k,)), dma((k,)),
-    ]
+    ] + [pltpu.VMEM((n, 8, 128), F32)] * with_full + [dma((5,))] + [dma((k,))] * 5
 
 
 def whole(dest, x_hbm, y_hbm, q_hbm, r_out, w_out, c_out, xin, yin, xo, yo, xr, yr, sr, xs, qv, acc, M, W, R, wp, wk, rk,
@@ -384,7 +382,10 @@
         for j in range(i, 4):
             gsum[0][16 * b:16 * b + 16] = acc[128 * i:128 * i + 128, 128 * j:128 * j + 128].reshape(16, 8, 128)
             b += 1
-    drain_g = all_sum(G_GROUPS, *gsum, after_z=later_y)
+    def store_half(src, dst):
+        dst[...] = src[...]
+
+    drain_g = all_sum(G_GROUPS, *gsum, keep=store_half, after_z=later_y)
     loop(EARLY, CHUNKS, forward)
     full = gsum[7]
     b = 0
@@ -394,7 +395,7 @@
             b += 1
     factor(M, R, W, wk, rk)
     out_r = pltpu.make_async_copy(R, r_out, osem.at[0])
-    out_w = pltpu.make_async_copy(wp, w_out, osem.at[1])
+    out_w = pltpu.make_async_copy(wp.at[0:2], w_out, osem.at[1])
     out_r.start()
     wp[0] = W[...].astype(BF16)
     wp[1] = (W[...] - wp[0].astype(F32)).astype(BF16)
@@ -436,9 +437,11 @@
     loop(0, CHUNKS, cross_step)
     for j in range(4):
         csum[0][64 * j:64 * j + 64] = acc[:, 128 * j:128 * j + 128].reshape(64, 8, 128)
-    drain_c = all_sum(C_GROUPS, *csum, after_scatter=form_basis)
-    out_c = pltpu.make_async_copy(csum[7], c_out, osem.at[2])
-    out_c.start()
+
+    def copy_half(src, dst):
+        pltpu.make_async_copy(src, dst, osem.at[2]).start()
+
+    drain_c = all_sum(C_GROUPS, *csum[:7], c_out, *csum[7:], keep=copy_half, after_scatter=form_basis)
     drain_g()
     drain_c()
     await_bytes(ids.at[0:31], id_s.at[0])
@@ -448,7 +451,7 @@
     loop(0, 4, lambda i: store_q(i).wait())
     out_r.wait()
     out_w.wait()
-    out_c.wait()
+    await_bytes(csum[2], osem.at[2])
 
 
 def finish(q_in, r_in, w_in, c_in, q_out, r_out, p_out, qv, R, W, C, cp, p, qi, qo, ii, oo):
@@ -470,10 +473,8 @@
         rows = C[64 * j:64 * j + 64].reshape(512, 128)
         span = slice(128 * j, 128 * j + 128)
         c1 = rows.astype(BF16)
-        c2 = (rows - c1.astype(F32)).astype(BF16)
         cp[0, :, span] = c1
-        cp[1, :, span] = c2
-        cp[2, :, span] = (rows - c1.astype(F32) - c2.astype(F32)).astype(BF16)
+        cp[1, :, span] = (rows - c1.astype(F32)).astype(BF16)
     get_w.wait()
 
     def term(i, j):
@@ -482,7 +483,7 @@
     for i in range(2):
         gets[i].wait()
         puts[i].start()
-    p[...] = (term(2, 0) + term(0, 2) + term(1, 1) + term(1, 0) + term(0, 1) + term(0, 0)) * (1.0 / 512.0)
+    p[...] = (term(1, 1) + term(1, 0) + term(0, 1) + term(0, 0)) * (1.0 / 512.0)
     put_p.start()
     for i in range(2, 4):
         gets[i].wait()
@@ -503,7 +504,7 @@
     panels = pltpu.VMEM((4, 128, 32, 128), BF16)
     basis, upper, inverse, cross = pl.pallas_call(
         whole,
-        out_shape=(jax.ShapeDtypeStruct((BLK_DEV, 32, 512), F32), square, jax.ShapeDtypeStruct((3, 512, 512), BF16), jax.ShapeDtypeStruct((CT, 8, 128), F32)),
+        out_shape=(jax.ShapeDtypeStruct((BLK_DEV, 32, 512), F32), square, jax.ShapeDtypeStruct((2, 512, 512), BF16), jax.ShapeDtypeStruct((CT, 8, 128), F32)),
         in_specs=[V, A, A],
         out_specs=(A, A, A, A),
         scratch_shapes=[
@@ -527,7 +528,7 @@
             dma((2,)), dma((2,)), dma((4,)), dma((3,)),
             dma((1,)), dma((CHUNKS,)), dma((1,)), dma((CHUNKS,)),
             dma((1,)), dma((1,)), dma((1,)), dma((1,)),
-        ] + sum_scratch(G_GROUPS) + sum_scratch(C_GROUPS),
+        ] + sum_scratch(G_GROUPS, True) + sum_scratch(C_GROUPS, False),
         compiler_params=pltpu.CompilerParams(
             collective_id=0, has_side_effects=True, vmem_limit_bytes=63 << 20
         ),
@@ -541,9 +542,9 @@
         scratch_shapes=[
             pltpu.VMEM((BLK_DEV, 32, 512), F32),
             pltpu.VMEM((512, 512), F32),
-            pltpu.VMEM((3, 512, 512), BF16),
+            pltpu.VMEM((2, 512, 512), BF16),
             pltpu.VMEM((CT, 8, 128), F32),
-            pltpu.VMEM((3, 512, 512), BF16),
+            pltpu.VMEM((2, 512, 512), BF16),
             pltpu.VMEM((512, 512), F32),
             dma((4,)), dma((4,)), dma((3,)), dma((2,)),
         ],

time: 135 us -> 133 us (0.985)
  no operation moved by 1% of the time
where the time goes in v5:
time: 133 us
  Pallas kernels  133 us (100%)
    pallas_call x1, Pallas kernels, body(): pl.pallas_call(whole, out_shape=(jax.ShapeDtypeStruct((BLK_DEV, 32, 512),...  127 us
    pallas_call x1, Pallas kernels, body(): pl.pallas_call(finish, out_shape=(jax.ShapeDtypeStruct((BLK_DEV, 32, 512)...  5.51 us

profile of v5, /device:TPU:1, one launch (start us, length us, event | category | flops | bytes accessed | tf_op | source)
XLA Modules:
  0.0 133.2 jit_solution(2582856207253341324)
XLA Ops:
  0.6 127.1 %window.1 = (f32[64,32,512]{2,1,0:T(8,128)}, f32[512,512]{1,0:T(8,128)}, bf16[2,512,512]{2,1,0:T(8,128)(2,1)}, f32[256,8,128]{2,1,0:T(8,128)}) custom-call(s32[1,128]{1,0:T(1,128)} %bitcast.1, bf16[128,128,128]{2,1,0:T(8,128)(2,1)} %x_hbm.1, bf16[128,128,128]{2,1,0:T(8,128)(2,1)} %y_hbm.1), custom_call_target="tpu_custom_call" | custom-call | tf_op jit(solution)/shard_map/window/pallas_call | solution.py:505
  127.7 5.5 %finish.1 = (f32[64,32,512]{2,1,0:T(8,128)}, f32[512,512]{1,0:T(8,128)}, f32[512,512]{1,0:T(8,128)}) custom-call(f32[64,32,512]{2,1,0:T(8,128)} %get-tuple-element.7.q_in, f32[512,512]{1,0:T(8,128)} %get-tuple-element.8.r_in, bf16[2,512,512]{2,1,0:T(8,128)(2,1)} %get-tuple-element.9.w_in, f32[256,8,128]{2,1,0:T(8,128)} %get-tuple-element.10.c_in), custom_call_target="tpu_custom_call" | custom-call | tf_op jit(solution)/shard_map/finish/pallas_call | solution.py:537

commit v6 on v5

--- a/solution.py
+++ b/solution.py
@@ -455,45 +455,48 @@
 
 
 def finish(q_in, r_in, w_in, c_in, q_out, r_out, p_out, qv, R, W, C, cp, p, qi, qo, ii, oo):
-    get_c = pltpu.make_async_copy(c_in, C, ii.at[0])
+    halves = [pl.ds(128 * i, 128) for i in range(2)]
+    get_c = [pltpu.make_async_copy(c_in.at[t], C.at[t], ii.at[3 * i]) for i, t in enumerate(halves)]
     get_w = pltpu.make_async_copy(w_in, W, ii.at[1])
     get_r = pltpu.make_async_copy(r_in, R, ii.at[2])
     parts = [pl.ds(16 * i, 16) for i in range(4)]
     gets = [pltpu.make_async_copy(q_in.at[t], qv.at[t], qi.at[i]) for i, t in enumerate(parts)]
     puts = [pltpu.make_async_copy(qv.at[t], q_out.at[t], qo.at[i]) for i, t in enumerate(parts)]
     put_r = pltpu.make_async_copy(R, r_out, oo.at[0])
-    put_p = pltpu.make_async_copy(p, p_out, oo.at[1])
-    get_c.start()
+    sides = [slice(0, 256), slice(256, 512)]
+    put_p = [pltpu.make_async_copy(p.at[:, t], p_out.at[:, t], oo.at[1 + i]) for i, t in enumerate(sides)]
+    get_c[0].start()
     get_w.start()
+    get_c[1].start()
     for copy in gets:
         copy.start()
     get_r.start()
-    get_c.wait()
-    for j in range(4):
-        rows = C[64 * j:64 * j + 64].reshape(512, 128)
-        span = slice(128 * j, 128 * j + 128)
-        c1 = rows.astype(BF16)
-        cp[0, :, span] = c1
-        cp[1, :, span] = (rows - c1.astype(F32)).astype(BF16)
-    get_w.wait()
-
-    def term(i, j):
-        return jnp.dot(W[i], cp[j], preferred_element_type=F32)
-
     for i in range(2):
-        gets[i].wait()
-        puts[i].start()
-    p[...] = (term(1, 1) + term(1, 0) + term(0, 1) + term(0, 0)) * (1.0 / 512.0)
-    put_p.start()
-    for i in range(2, 4):
-        gets[i].wait()
-        puts[i].start()
+        get_c[i].wait()
+        for j in (2 * i, 2 * i + 1):
+            rows = C[64 * j:64 * j + 64].reshape(512, 128)
+            span = slice(128 * j, 128 * j + 128)
+            c1 = rows.astype(BF16)
+            cp[0, :, span] = c1
+            cp[1, :, span] = (rows - c1.astype(F32)).astype(BF16)
+        if i == 0:
+            get_w.wait()
+
+        def term(a, b):
+            return jnp.dot(W[a], cp[b, :, sides[i]], preferred_element_type=F32)
+
+        p[:, sides[i]] = (term(1, 1) + term(1, 0) + term(0, 1) + term(0, 0)) * (1.0 / 512.0)
+        put_p[i].start()
+        for t in (2 * i, 2 * i + 1):
+            gets[t].wait()
+            puts[t].start()
     get_r.wait()
     put_r.start()
     for copy in puts:
         copy.wait()
     put_r.wait()
-    put_p.wait()
+    for copy in put_p:
+        copy.wait()
 
 
 def body(owned_x, owned_y, patch_dest):
@@ -546,7 +549,7 @@
             pltpu.VMEM((CT, 8, 128), F32),
             pltpu.VMEM((2, 512, 512), BF16),
             pltpu.VMEM((512, 512), F32),
-            dma((4,)), dma((4,)), dma((3,)), dma((2,)),
+            dma((4,)), dma((4,)), dma((4,)), dma((3,)),
         ],
         compiler_params=pltpu.CompilerParams(vmem_limit_bytes=63 << 20),
         name="finish",

time: 133 us -> 134 us (level)
  no operation moved by 1% of the time
where the time goes in v6:
time: 134 us
  Pallas kernels  133 us (99%)
    pallas_call x1, Pallas kernels, body(): pl.pallas_call(whole, out_shape=(jax.ShapeDtypeStruct((BLK_DEV, 32, 512),...  127 us
    pallas_call x1, Pallas kernels, body(): pl.pallas_call(finish, out_shape=(jax.ShapeDtypeStruct((BLK_DEV, 32, 512)...  6.15 us

profile of v6, /device:TPU:1, one launch (start us, length us, event | category | flops | bytes accessed | tf_op | source)
XLA Modules:
  0.0 133.8 jit_solution(7800371588989700079)
XLA Ops:
  0.6 127.1 %window.1 = (f32[64,32,512]{2,1,0:T(8,128)}, f32[512,512]{1,0:T(8,128)}, bf16[2,512,512]{2,1,0:T(8,128)(2,1)}, f32[256,8,128]{2,1,0:T(8,128)}) custom-call(s32[1,128]{1,0:T(1,128)} %bitcast.1, bf16[128,128,128]{2,1,0:T(8,128)(2,1)} %x_hbm.1, bf16[128,128,128]{2,1,0:T(8,128)(2,1)} %y_hbm.1), custom_call_target="tpu_custom_call" | custom-call | tf_op jit(solution)/shard_map/window/pallas_call | solution.py:508
  127.7 6.2 %finish.1 = (f32[64,32,512]{2,1,0:T(8,128)}, f32[512,512]{1,0:T(8,128)}, f32[512,512]{1,0:T(8,128)}) custom-call(f32[64,32,512]{2,1,0:T(8,128)} %get-tuple-element.7.q_in, f32[512,512]{1,0:T(8,128)} %get-tuple-element.8.r_in, bf16[2,512,512]{2,1,0:T(8,128)(2,1)} %get-tuple-element.9.w_in, f32[256,8,128]{2,1,0:T(8,128)} %get-tuple-element.10.c_in), custom_call_target="tpu_custom_call" | custom-call | tf_op jit(solution)/shard_map/finish/pallas_call | solution.py:540
